TPU v7x, 128 devices: a whole 4x4x4 slice. The times are simulated.
128 devices in a mesh: space: 32 (over x, y, z_hi), shot: 4 (over z_lo, core).
Axes of the slice: x: 4, y: 4, z: 4 (z_hi: 2, z_lo: 2; z = z_hi * 2 + z_lo), core: 2. Of those that a mesh axis runs over, the one named last changes fastest.
Arguments:
- adjoint_state: float32 [4, 9, 128, 128, 256], P('shot', None, 'space'), may hold values from -6 to 6
- forward_strain: bfloat16 [4, 4, 6, 128, 128, 256], P('shot', None, None, 'space'), may hold values from -6 to 6
- traces: float32 [4, 4, 256], P('shot'), may hold values from -12 to 12
- receivers: int32 [4, 256], P('shot'), may hold values from 0 to 4194303
- sections: int32 [32], replicated, may hold values from 0 to 1
- lame_lambda: float32 [128, 128, 256], P('space'), may hold values from 1 to 2
- lame_mu: float32 [128, 128, 256], P('space'), may hold values from 0.3 to 1
- buoyancy: float32 [128, 128, 256], P('space'), may hold values from 0.5 to 1
Outputs:
- final_state: float32 [4, 9, 128, 128, 256], P('shot', None, 'space')
- model_new: float32 [2, 128, 128, 256], P(None, 'space')
Inputs may be any that keep to these rules, and one draw needn't show every extreme that they name: `sections`: 0 marks a water slab, 1 a solid one. A receiver's flat cell index is x * 128 * 256 + y * 256 + z; several receivers may share a cell.
All inputs are finite; a program needn't handle non-finite values. Where the computation divides by a largest or mean magnitude, that divisor is 1e-20 or more.
Results may differ from a plain program's by a relative error of at most 0.0003.
Values sent between devices are 32-bit elements; how exact they have to be, the bound alone decides.
No kernel may reach another device: no remote copies, remote signals or barrier semaphores. Data moves between devices by JAX's collectives and lax.ppermute only.
A program may use at most 128 MiB of HBM per device.

v0:
```python
import jax
import jax.numpy as jnp
from jax import lax
from jax.sharding import PartitionSpec as P

STEPS = 4


COURANT = 0.15
RATE = 0.2
EPS = 1e-06


def shifted(block, axis, distance):
    devices = range(lax.axis_size(axis))
    route = [(i - distance, i) for i in devices if i - distance in devices]
    return lax.ppermute(block, axis, route)


def back_diff(field, axis):
    count = field.shape[axis]
    earlier = jnp.concatenate(
        [
            jnp.zeros_like(lax.slice_in_dim(field, 0, 1, axis=axis)),
            lax.slice_in_dim(field, 0, count - 1, axis=axis),
        ],
        axis=axis,
    )
    return field - earlier


def fore_diff(field, axis):
    count = field.shape[axis]
    later = jnp.concatenate(
        [
            lax.slice_in_dim(field, 1, count, axis=axis),
            jnp.zeros_like(lax.slice_in_dim(field, 0, 1, axis=axis)),
        ],
        axis=axis,
    )
    return later - field


def back_plane(field, plane):
    return field - jnp.concatenate([plane[None], field[:-1]], axis=0)


def fore_plane(field, plane):
    return jnp.concatenate([field[1:], plane[None]], axis=0) - field


def shards(
    adjoint_state, forward_strain, traces, receivers, sections, lame_lambda, lame_mu, buoyancy
):
    state = adjoint_state[0]
    strains = forward_strain[0]
    shot_traces = traces[0]
    shot_recv = receivers[0]
    shape = lame_lambda.shape
    cells = shape[0] * shape[1] * shape[2]
    slab = lax.axis_index("space")
    solid_flag = lax.dynamic_index_in_dim(sections, slab, keepdims=False)
    solid_value = solid_flag.astype(jnp.float32)
    shear = lame_mu * solid_value
    local_index = shot_recv - slab * cells
    inside = (local_index >= 0) & (local_index < cells)
    placed = jnp.where(inside, local_index, 0)
    velocity = [state[0], state[1], state[2]]
    stress = [state[3 + k] for k in range(6)]
    grad_lam = jnp.zeros(shape, jnp.float32)
    grad_shear = jnp.zeros(shape, jnp.float32)

    def elastic(operands):
        stress_in, grad_lam_in, grad_shear_in, vel, right, fwd = operands
        strain_xx = fore_plane(vel[0], right[0])
        strain_yy = fore_diff(vel[1], 1)
        strain_zz = fore_diff(vel[2], 2)
        shear_xy = fore_diff(vel[0], 1) + fore_plane(vel[1], right[1])
        shear_xz = fore_diff(vel[0], 2) + fore_plane(vel[2], right[2])
        shear_yz = fore_diff(vel[1], 2) + fore_diff(vel[2], 1)
        diverge = strain_xx + strain_yy + strain_zz
        updated = [
            stress_in[0] + COURANT * (lame_lambda * diverge + 2.0 * shear * strain_xx),
            stress_in[1] + COURANT * (lame_lambda * diverge + 2.0 * shear * strain_yy),
            stress_in[2] + COURANT * (lame_lambda * diverge + 2.0 * shear * strain_zz),
            stress_in[3] + COURANT * shear * shear_xy,
            stress_in[4] + COURANT * shear * shear_xz,
            stress_in[5] + COURANT * shear * shear_yz,
        ]
        new_lam = grad_lam_in + diverge * (fwd[0] + fwd[1] + fwd[2])
        new_shear = grad_shear_in + solid_value * (
            2.0 * (strain_xx * fwd[0] + strain_yy * fwd[1] + strain_zz * fwd[2])
            + shear_xy * fwd[3]
            + shear_xz * fwd[4]
            + shear_yz * fwd[5]
        )
        return (tuple(updated), new_lam, new_shear)

    def acoustic(operands):
        stress_in, grad_lam_in, grad_shear_in, vel, right, fwd = operands
        diverge = fore_plane(vel[0], right[0]) + fore_diff(vel[1], 1) + fore_diff(vel[2], 2)
        pressure_step = COURANT * (lame_lambda * diverge)
        updated = (
            stress_in[0] + pressure_step,
            stress_in[1] + pressure_step,
            stress_in[2] + pressure_step,
            stress_in[3],
            stress_in[4],
            stress_in[5],
        )
        new_lam = grad_lam_in + diverge * (fwd[0] + fwd[1] + fwd[2])
        return (updated, new_lam, grad_shear_in)

    for step in range(STEPS):
        amount = jnp.where(inside, shot_traces[step], 0.0)
        left = shifted(jnp.stack([stress[0][-1], stress[3][-1], stress[4][-1]]), "space", 1)
        velocity[0] = velocity[0] + COURANT * buoyancy * (
            back_plane(stress[0], left[0]) + back_diff(stress[3], 1) + back_diff(stress[4], 2)
        )
        velocity[1] = velocity[1] + COURANT * buoyancy * (
            back_plane(stress[3], left[1]) + back_diff(stress[1], 1) + back_diff(stress[5], 2)
        )
        velocity[2] = velocity[2] + COURANT * buoyancy * (
            back_plane(stress[4], left[2]) + back_diff(stress[5], 1) + back_diff(stress[2], 2)
        )
        velocity[2] = velocity[2].reshape(-1).at[placed].add(amount).reshape(shape)
        right = shifted(jnp.stack([velocity[0][0], velocity[1][0], velocity[2][0]]), "space", -1)
        fwd = strains[step].astype(jnp.float32)
        operands = (tuple(stress), grad_lam, grad_shear, tuple(velocity), right, fwd)
        new_stress, grad_lam, grad_shear = lax.cond(solid_flag == 1, elastic, acoustic, operands)
        stress = list(new_stress)
    final_state = jnp.stack(velocity + stress)[None]
    gradients = jnp.stack([grad_lam, grad_shear])
    model_pair = jnp.stack([lame_lambda, lame_mu])
    totals = lax.psum(gradients, "shot")
    peak_lam, peak_mu = lax.pmax(
        (jnp.max(jnp.abs(totals[0])), jnp.max(jnp.abs(totals[1]))), "space"
    )
    peaks = jnp.stack([peak_lam, peak_mu])
    model_new = model_pair * (1.0 - RATE * totals / (peaks[:, None, None, None] + EPS))
    return (final_state, model_new)


def solution(mesh):
    return jax.shard_map(
        shards,
        mesh=mesh,
        in_specs=(
            P("shot", None, "space", None, None),
            P("shot", None, None, "space", None, None),
            P("shot", None, None),
            P("shot", None),
            P(),
            P("space", None, None),
            P("space", None, None),
            P("space", None, None),
        ),
        out_specs=(P("shot", None, "space", None, None), P(None, "space", None, None)),
        check_vma=False,
    )
```

profile of v0, /device:TPU:0, one launch (start us, length us, event | category | flops | bytes accessed | tf_op | source)
XLA Modules:
  0.0 353.8 jit_solution(6022568969430405890)
XLA Ops:
  9.0 5.9 %collective-permute-start = (f32[3,128,256]{2,1,0:T(8,128)}, f32[3,128,256]{2,1,0:T(8,128)S(1)}, u32[]{:S(2)}, u32[]{:S(2)}) collective-permute-start(f32[3,128,256]{2,1,0:T(8,128)} %pad_maximum_fusion.1), channel_id=1, source_target_pairs={{0,4},{4,8},{8,12},{12,16},{16,20},{20,24},{24,28},{28,32},{32,36}... | collective-permute-start | bytes 1179656 | tf_op jit(solution)/shard_map/ppermute | solution.py:17
  15.0 2.2 slice_bitcast_fusion.7
  20.1 2.9 slice_bitcast_fusion.5
  24.6 2.7 scatter_fusion
  28.1 1.9 fusion.52
  30.9 1.4 collective-permute-start.1
  32.3 8.2 %bitcast_convert_fusion = (f32[6,4,128,256]{3,2,1,0:T(8,128)}, f32[6,4,128,256]{3,2,1,0:T(8,128)}, f32[6,4,128,256]{3,2,1,0:T(8,128)}, f32[6,4,128,256]{3,2,1,0:T(8,128)}) fusion(bf16[1,4,6,4,128,256]{5,4,3,2,1,0:T(8,128)(2,1)} %param.17), kind=kLoop, calls=%fused_computation.131 | loop fusion | flops 3145728 | bytes 18874368 | tf_op jit(solution)/shard_map/convert_element_type | solution.py:128
  40.6 1.2 dynamic_slice.4
  43.1 1.9 broadcast_multiply_fusion
  44.9 2.0 reshape.186
  46.9 7.1 %conditional.4 = (f32[4,128,256]{2,1,0:T(8,128)S(1)}, f32[4,128,256]{2,1,0:T(8,128)S(1)}, f32[4,128,256]{2,1,0:T(8,128)S(1)}, f32[4,128,256]{2,1,0:T(8,128)S(1)}...) conditional(s32[]{:T(128)} %bitcast.32, ...), branch_computations={%region_1.2_spmd, %region_2.3_spmd} | conditional | flops 7077888 | bytes 52363448 | solution.py:130
  48.3 1.2 slice.674
  52.3 1.8 multiply_add_fusion.1
  54.1 1.3 multiply_add_fusion.32
  55.5 6.4 %collective-permute-start.2 = (f32[3,128,256]{2,1,0:T(8,128)S(1)}, f32[3,128,256]{2,1,0:T(8,128)S(1)}, u32[]{:S(2)}, u32[]{:S(2)}) collective-permute-start(f32[3,128,256]{2,1,0:T(8,128)S(1)} %pad_maximum_fusion.3), channel_id=1, source_target_pairs={{0,4},{4,8},{8,12},{12,16},{16,20},{20,24},{24,28},{28,32},{32,36}... | collective-permute-start | bytes 1179656 | tf_op jit(solution)/shard_map/ppermute | solution.py:17
  62.3 7.1 %collective-permute-done.2 = f32[3,128,256]{2,1,0:T(8,128)S(1)} collective-permute-done((f32[3,128,256]{2,1,0:T(8,128)S(1)}, f32[3,128,256]{2,1,0:T(8,128)S(1)}, u32[]{:S(2)}, u32[]{:S(2)}) %collective-permute-start.2) | collective-permute-done | bytes 393248 | tf_op jit(solution)/shard_map/ppermute | solution.py:17
  72.5 4.1 %scatter_fusion.1 = f32[131072]{0:T(1024)} fusion(f32[131072]{0:T(1024)} %bitcast.311, s32[256]{0:T(256)S(1)} %bitcast.328, f32[256]{0:T(256)S(1)} %get-tuple-element.1114), kind=kCustom, calls=%fused_computation.1 | custom fusion | flops 256 | bytes 4096 | tf_op jit(solution)/shard_map/scatter-add | solution.py:126
  78.4 1.3 collective-permute-start.3
  79.7 2.4 bitcast_multiply_fusion.27
  82.1 2.0 reshape.188
  84.1 7.8 %collective-permute-done.3 = f32[3,128,256]{2,1,0:T(8,128)S(1)} collective-permute-done((f32[3,128,256]{2,1,0:T(8,128)}, f32[3,128,256]{2,1,0:T(8,128)S(1)}, u32[]{:S(2)}, u32[]{:S(2)}) %collective-permute-start.3) | collective-permute-done | bytes 393248 | tf_op jit(solution)/shard_map/ppermute | solution.py:17
  91.9 7.2 %conditional.5 = (f32[4,128,256]{2,1,0:T(8,128)S(1)}, f32[4,128,256]{2,1,0:T(8,128)S(1)}, f32[4,128,256]{2,1,0:T(8,128)S(1)}, f32[4,128,256]{2,1,0:T(8,128)}, f3...) conditional(s32[]{:T(128)} %bitcast.32, ...), branch_computations={%region_4.5_spmd, %region_5.6_spmd} | conditional | flops 7208960 | bytes 57082104 | solution.py:130
  93.2 1.3 slice.696
  97.3 1.8 multiply_add_fusion.7
  99.1 1.2 multiply_add_fusion.29
  100.4 6.7 %collective-permute-start.4 = (f32[3,128,256]{2,1,0:T(8,128)S(1)}, f32[3,128,256]{2,1,0:T(8,128)S(1)}, u32[]{:S(2)}, u32[]{:S(2)}) collective-permute-start(f32[3,128,256]{2,1,0:T(8,128)S(1)} %pad_maximum_fusion.5), channel_id=1, source_target_pairs={{0,4},{4,8},{8,12},{12,16},{16,20},{20,24},{24,28},{28,32},{32,36}... | collective-permute-start | bytes 1179656 | tf_op jit(solution)/shard_map/ppermute | solution.py:17
  108.4 4.4 %collective-permute-done.4 = f32[3,128,256]{2,1,0:T(8,128)S(1)} collective-permute-done((f32[3,128,256]{2,1,0:T(8,128)S(1)}, f32[3,128,256]{2,1,0:T(8,128)S(1)}, u32[]{:S(2)}, u32[]{:S(2)}) %collective-permute-start.4) | collective-permute-done | bytes 393248 | tf_op jit(solution)/shard_map/ppermute | solution.py:17
  115.9 4.1 %scatter_fusion.2 = f32[131072]{0:T(1024)} fusion(f32[131072]{0:T(1024)} %bitcast.312, s32[256]{0:T(256)S(1)} %bitcast.329, f32[256]{0:T(256)S(1)} %get-tuple-element.1113), kind=kCustom, calls=%fused_computation.2 | custom fusion | flops 256 | bytes 4096 | tf_op jit(solution)/shard_map/scatter-add | solution.py:126
  121.8 1.3 collective-permute-start.5
  123.1 2.6 fusion.100
  125.7 2.0 reshape.190
  127.7 5.9 %collective-permute-done.5 = f32[3,128,256]{2,1,0:T(8,128)S(1)} collective-permute-done((f32[3,128,256]{2,1,0:T(8,128)}, f32[3,128,256]{2,1,0:T(8,128)S(1)}, u32[]{:S(2)}, u32[]{:S(2)}) %collective-permute-start.5) | collective-permute-done | bytes 393248 | tf_op jit(solution)/shard_map/ppermute | solution.py:17
  133.6 7.1 %conditional.6 = (f32[4,128,256]{2,1,0:T(8,128)S(1)}, f32[4,128,256]{2,1,0:T(8,128)S(1)}, f32[4,128,256]{2,1,0:T(8,128)S(1)}, f32[4,128,256]{2,1,0:T(8,128)}, f3...) conditional(s32[]{:T(128)} %bitcast.32, ...), branch_computations={%region_7.8_spmd, %region_8.9_spmd} | conditional | flops 7208960 | bytes 57082104 | solution.py:130
  135.0 1.3 slice.718
  139.0 1.8 multiply_add_fusion.13
  140.8 1.2 multiply_add_fusion.26
  142.1 6.6 %collective-permute-start.6 = (f32[3,128,256]{2,1,0:T(8,128)S(1)}, f32[3,128,256]{2,1,0:T(8,128)S(1)}, u32[]{:S(2)}, u32[]{:S(2)}) collective-permute-start(f32[3,128,256]{2,1,0:T(8,128)S(1)} %pad_maximum_fusion.7), channel_id=1, source_target_pairs={{0,4},{4,8},{8,12},{12,16},{16,20},{20,24},{24,28},{28,32},{32,36}... | collective-permute-start | bytes 1179656 | tf_op jit(solution)/shard_map/ppermute | solution.py:17
  148.7 1.9 multiply_add_fusion.25
  151.6 2.2 collective-permute-done.6
  156.0 4.1 %scatter_fusion.3 = f32[131072]{0:T(1024)} fusion(f32[131072]{0:T(1024)} %bitcast.308, s32[256]{0:T(256)S(1)} %bitcast.330, f32[256]{0:T(256)S(1)} %get-tuple-element.1112), kind=kCustom, calls=%fused_computation.3 | custom fusion | flops 256 | bytes 4096 | tf_op jit(solution)/shard_map/scatter-add | solution.py:126
  160.1 1.6 slice.1012
  161.7 1.6 slice.961
  163.3 2.5 bitcast_dynamic-update-slice_fusion.7
  167.9 1.3 collective-permute-start.7
  169.2 2.1 fusion.99
  171.3 2.0 reshape.192
  173.3 2.0 stack_reshape.3
  175.3 1.9 constant_dynamic-update-slice_fusion
  177.2 2.6 collective-permute-done.7
  179.8 9.5 %conditional.7 = (f32[4,128,256]{2,1,0:T(8,128)S(1)}, f32[4,128,256]{2,1,0:T(8,128)S(1)}, f32[4,128,256]{2,1,0:T(8,128)S(1)}, f32[4,128,256]{2,1,0:T(8,128)}, f3...) conditional(s32[]{:T(128)} %bitcast.32, ...), branch_computations={%region_10.11_spmd, %region_11.12_spmd} | conditional | flops 7208960 | bytes 57082104 | solution.py:130
  181.0 1.4 slice.731
  182.4 1.2 slice.740
  185.1 1.4 multiply_add_fusion.18
  186.5 2.8 multiply_add_fusion.19
  189.3 1.9 fusion.98
  191.2 2.1 pad_maximum_fusion
  193.4 1.9 bitcast_dynamic-update-slice_fusion.5
  195.3 2.0 bitcast_dynamic-update-slice_fusion.4
  197.2 2.1 bitcast_dynamic-update-slice_fusion.3
  201.8 42.7 %all-reduce.59.cloned.1.call-done = f32[2,4,128,256]{3,2,1,0:T(8,128)} async-done(((f32[2,4,128,256]{3,2,1,0:T(8,128)}), f32[2,4,128,256]{3,2,1,0:T(8,128)}) %all-reduce.59.cloned.1.call-update) | async-done | bytes 1048592 | tf_op jit(solution)/shard_map/psum | solution.py:135
  244.6 1.9 fusion.48
  246.5 96.8 %all-reduce.56 = (f32[1]{0:T(128)}, f32[1]{0:T(128)}) all-reduce(f32[1]{0:T(128)} %bitcast.73, f32[1]{0:T(128)} %bitcast.72), channel_id=1, replica_groups=mesh['space'=32,'shot'=4] {'space'}, use_global_device_ids=true, to_apply=%region_16.17 | all-reduce | flops 2 | bytes 16 | tf_op jit(solution)/shard_map/pmax | solution.py:136
  343.3 1.3 maximum_add_fusion
  344.6 2.4 maximum_multiply_fusion
  (234 shorter events, 41.6 us)
Async XLA Ops:
  7.2 237.4 %all-reduce.59.cloned.1.call-start = ((), (), s32[]{:S(2)}) async-start(), calls=%async_computation | async-start | bytes 2097152 | tf_op jit(solution)/shard_map/psum | solution.py:135
  9.0 14.6 %collective-permute-start = (f32[3,128,256]{2,1,0:T(8,128)}, f32[3,128,256]{2,1,0:T(8,128)S(1)}, u32[]{:S(2)}, u32[]{:S(2)}) collective-permute-start(f32[3,128,256]{2,1,0:T(8,128)} %pad_maximum_fusion.1), channel_id=1, source_target_pairs={{0,4},{4,8},{8,12},{12,16},{16,20},{20,24},{24,28},{28,32},{32,36}... | collective-permute-start | bytes 1179656 | tf_op jit(solution)/shard_map/ppermute | solution.py:17
  15.0 8.7 %copy-start.6 = (f32[4,128,256]{2,1,0:T(8,128)S(1)}, f32[4,128,256]{2,1,0:T(8,128)}, u32[]{:S(2)}) copy-start(f32[4,128,256]{2,1,0:T(8,128)} %param.23) | copy-start | bytes 1572868
  18.0 5.7 %copy-start.24 = (f32[1,9,4,128,256]{4,3,2,1,0:T(8,128)S(1)}, f32[1,9,4,128,256]{4,3,2,1,0:T(8,128)}, u32[]{:S(2)}) copy-start(f32[1,9,4,128,256]{4,3,2,1,0:T(8,128)} %param.16) | copy-start | bytes 14155780
  23.0 1.6 copy-start.51
  23.0 1.6 copy-start.53
  30.9 16.0 %copy-start = (f32[4,128,256]{2,1,0:T(8,128)S(1)}, f32[4,128,256]{2,1,0:T(8,128)}, u32[]{:S(2)}) copy-start(f32[4,128,256]{2,1,0:T(8,128)} %param.21) | copy-start | bytes 1572868
  30.9 16.0 %collective-permute-start.1 = (f32[3,128,256]{2,1,0:T(8,128)}, f32[3,128,256]{2,1,0:T(8,128)S(1)}, u32[]{:S(2)}, u32[]{:S(2)}) collective-permute-start(f32[3,128,256]{2,1,0:T(8,128)} %pad_maximum_fusion.2), channel_id=1, source_target_pairs={{4,0},{8,4},{12,8},{16,12},{20,16},{24,20},{28,24},{32,28},{36,32}... | collective-permute-start | bytes 1179656 | tf_op jit(solution)/shard_map/ppermute | solution.py:17
  46.9 2.6 copy-start.18
  46.9 3.1 copy-start.29
  54.0 15.4 %copy-start.30 = (f32[4,128,256]{2,1,0:T(8,128)}, f32[4,128,256]{2,1,0:T(8,128)S(1)}, u32[]{:S(2)}) copy-start(f32[4,128,256]{2,1,0:T(8,128)S(1)} %get-tuple-element.960) | copy-start | bytes 1572868
  54.1 8.0 %copy-start.52 = (f32[4,128,256]{2,1,0:T(8,128)S(1)}, f32[4,128,256]{2,1,0:T(8,128)}, u32[]{:S(2)}) copy-start(f32[4,128,256]{2,1,0:T(8,128)} %get-tuple-element.955) | copy-start | bytes 1572868
  54.1 8.0 %copy-start.54 = (f32[4,128,256]{2,1,0:T(8,128)S(1)}, f32[4,128,256]{2,1,0:T(8,128)}, u32[]{:S(2)}) copy-start(f32[4,128,256]{2,1,0:T(8,128)} %get-tuple-element.958) | copy-start | bytes 1572868
  54.1 15.4 %copy-start.7 = (f32[4,128,256]{2,1,0:T(8,128)S(1)}, f32[4,128,256]{2,1,0:T(8,128)}, u32[]{:S(2)}) copy-start(f32[4,128,256]{2,1,0:T(8,128)} %param.23) | copy-start | bytes 1572868
  55.4 14.5 %copy-start.43 = (f32[4,128,256]{2,1,0:T(8,128)}, f32[4,128,256]{2,1,0:T(8,128)S(1)}, u32[]{:S(2)}) copy-start(f32[4,128,256]{2,1,0:T(8,128)S(1)} %multiply_add_fusion.32) | copy-start | bytes 1572868
  55.5 13.9 %collective-permute-start.2 = (f32[3,128,256]{2,1,0:T(8,128)S(1)}, f32[3,128,256]{2,1,0:T(8,128)S(1)}, u32[]{:S(2)}, u32[]{:S(2)}) collective-permute-start(f32[3,128,256]{2,1,0:T(8,128)S(1)} %pad_maximum_fusion.3), channel_id=1, source_target_pairs={{0,4},{4,8},{8,12},{12,16},{16,20},{20,24},{24,28},{28,32},{32,36}... | collective-permute-start | bytes 1179656 | tf_op jit(solution)/shard_map/ppermute | solution.py:17
  62.0 8.7 %copy-start.17 = (f32[4,128,256]{2,1,0:T(8,128)S(1)}, f32[4,128,256]{2,1,0:T(8,128)}, u32[]{:S(2)}) copy-start(f32[4,128,256]{2,1,0:T(8,128)} %reshape.186) | copy-start | bytes 1572868
  62.2 9.2 %copy-start.48 = (f32[4,128,256]{2,1,0:T(8,128)}, f32[4,128,256]{2,1,0:T(8,128)S(1)}, u32[]{:S(2)}) copy-start(f32[4,128,256]{2,1,0:T(8,128)S(1)} %get-tuple-element.1116) | copy-start | bytes 1572868
  62.3 9.2 %copy-start.50 = (f32[4,128,256]{2,1,0:T(8,128)}, f32[4,128,256]{2,1,0:T(8,128)S(1)}, u32[]{:S(2)}) copy-start(f32[4,128,256]{2,1,0:T(8,128)S(1)} %get-tuple-element.1117) | copy-start | bytes 1572868
  71.4 20.4 %copy-start.4 = (f32[4,128,256]{2,1,0:T(8,128)S(1)}, f32[4,128,256]{2,1,0:T(8,128)}, u32[]{:S(2)}) copy-start(f32[4,128,256]{2,1,0:T(8,128)} %copy-done.3) | copy-start | bytes 1572868
  78.4 13.5 %collective-permute-start.3 = (f32[3,128,256]{2,1,0:T(8,128)}, f32[3,128,256]{2,1,0:T(8,128)S(1)}, u32[]{:S(2)}, u32[]{:S(2)}) collective-permute-start(f32[3,128,256]{2,1,0:T(8,128)} %pad_maximum_fusion.4), channel_id=1, source_target_pairs={{4,0},{8,4},{12,8},{16,12},{20,16},{24,20},{28,24},{32,28},{36,32}... | collective-permute-start | bytes 1179656 | tf_op jit(solution)/shard_map/ppermute | solution.py:17
  91.9 2.6 copy-start.20
  91.9 3.1 copy-start.28
  91.9 3.1 copy-start.31
  95.9 3.1 copy-start.32
  99.0 9.3 %copy-start.49 = (f32[4,128,256]{2,1,0:T(8,128)S(1)}, f32[4,128,256]{2,1,0:T(8,128)}, u32[]{:S(2)}) copy-start(f32[4,128,256]{2,1,0:T(8,128)} %get-tuple-element.970) | copy-start | bytes 1572868
  99.1 13.9 %copy-start.5 = (f32[4,128,256]{2,1,0:T(8,128)S(1)}, f32[4,128,256]{2,1,0:T(8,128)}, u32[]{:S(2)}) copy-start(f32[4,128,256]{2,1,0:T(8,128)} %copy-done.3) | copy-start | bytes 1572868
  99.1 13.9 %copy-start.8 = (f32[4,128,256]{2,1,0:T(8,128)S(1)}, f32[4,128,256]{2,1,0:T(8,128)}, u32[]{:S(2)}) copy-start(f32[4,128,256]{2,1,0:T(8,128)} %param.23) | copy-start | bytes 1572868
  100.3 13.0 %copy-start.44 = (f32[4,128,256]{2,1,0:T(8,128)}, f32[4,128,256]{2,1,0:T(8,128)S(1)}, u32[]{:S(2)}) copy-start(f32[4,128,256]{2,1,0:T(8,128)S(1)} %multiply_add_fusion.29) | copy-start | bytes 1572868
  100.4 12.5 %collective-permute-start.4 = (f32[3,128,256]{2,1,0:T(8,128)S(1)}, f32[3,128,256]{2,1,0:T(8,128)S(1)}, u32[]{:S(2)}, u32[]{:S(2)}) collective-permute-start(f32[3,128,256]{2,1,0:T(8,128)S(1)} %pad_maximum_fusion.5), channel_id=1, source_target_pairs={{0,4},{4,8},{8,12},{12,16},{16,20},{20,24},{24,28},{28,32},{32,36}... | collective-permute-start | bytes 1179656 | tf_op jit(solution)/shard_map/ppermute | solution.py:17
  108.2 5.9 %copy-start.45 = (f32[4,128,256]{2,1,0:T(8,128)}, f32[4,128,256]{2,1,0:T(8,128)S(1)}, u32[]{:S(2)}) copy-start(f32[4,128,256]{2,1,0:T(8,128)S(1)} %multiply_add_fusion.28) | copy-start | bytes 1572868
  108.2 5.9 %copy-start.19 = (f32[4,128,256]{2,1,0:T(8,128)S(1)}, f32[4,128,256]{2,1,0:T(8,128)}, u32[]{:S(2)}) copy-start(f32[4,128,256]{2,1,0:T(8,128)} %reshape.188) | copy-start | bytes 1572868
  108.4 6.4 %copy-start.46 = (f32[4,128,256]{2,1,0:T(8,128)}, f32[4,128,256]{2,1,0:T(8,128)S(1)}, u32[]{:S(2)}) copy-start(f32[4,128,256]{2,1,0:T(8,128)S(1)} %multiply_add_fusion.27) | copy-start | bytes 1572868
  114.8 18.8 %copy-start.2 = (f32[4,128,256]{2,1,0:T(8,128)S(1)}, f32[4,128,256]{2,1,0:T(8,128)}, u32[]{:S(2)}) copy-start(f32[4,128,256]{2,1,0:T(8,128)} %copy-done.1) | copy-start | bytes 1572868
  121.8 11.8 %collective-permute-start.5 = (f32[3,128,256]{2,1,0:T(8,128)}, f32[3,128,256]{2,1,0:T(8,128)S(1)}, u32[]{:S(2)}, u32[]{:S(2)}) collective-permute-start(f32[3,128,256]{2,1,0:T(8,128)} %pad_maximum_fusion.6), channel_id=1, source_target_pairs={{4,0},{8,4},{12,8},{16,12},{20,16},{24,20},{28,24},{32,28},{36,32}... | collective-permute-start | bytes 1179656 | tf_op jit(solution)/shard_map/ppermute | solution.py:17
  133.6 2.6 copy-start.22
  133.6 3.1 copy-start.26
  133.6 3.1 copy-start.33
  137.7 3.1 copy-start.34
  140.8 10.7 %copy-start.47 = (f32[4,128,256]{2,1,0:T(8,128)S(1)}, f32[4,128,256]{2,1,0:T(8,128)}, u32[]{:S(2)}) copy-start(f32[4,128,256]{2,1,0:T(8,128)} %get-tuple-element.983) | copy-start | bytes 1572868
  140.8 13.7 %copy-start.9 = (f32[4,128,256]{2,1,0:T(8,128)S(1)}, f32[4,128,256]{2,1,0:T(8,128)}, u32[]{:S(2)}) copy-start(f32[4,128,256]{2,1,0:T(8,128)} %param.23) | copy-start | bytes 1572868
  140.8 13.7 %copy-start.21 = (f32[4,128,256]{2,1,0:T(8,128)S(1)}, f32[4,128,256]{2,1,0:T(8,128)}, u32[]{:S(2)}) copy-start(f32[4,128,256]{2,1,0:T(8,128)} %reshape.190) | copy-start | bytes 1572868
  142.0 8.6 %copy-start.38 = (f32[4,128,256]{2,1,0:T(8,128)}, f32[4,128,256]{2,1,0:T(8,128)S(1)}, u32[]{:S(2)}) copy-start(f32[4,128,256]{2,1,0:T(8,128)S(1)} %multiply_add_fusion.26) | copy-start | bytes 1572868
  142.1 11.6 %collective-permute-start.6 = (f32[3,128,256]{2,1,0:T(8,128)S(1)}, f32[3,128,256]{2,1,0:T(8,128)S(1)}, u32[]{:S(2)}, u32[]{:S(2)}) collective-permute-start(f32[3,128,256]{2,1,0:T(8,128)S(1)} %pad_maximum_fusion.7), channel_id=1, source_target_pairs={{0,4},{4,8},{8,12},{12,16},{16,20},{20,24},{24,28},{28,32},{32,36}... | collective-permute-start | bytes 1179656 | tf_op jit(solution)/shard_map/ppermute | solution.py:17
  151.6 3.4 copy-start.42
  151.6 11.7 %slice-start = ((f32[4,128,256]{2,1,0:T(8,128)}), f32[3,128,256]{2,1,0:T(8,128)S(1)}, s32[]{:S(2)}) async-start(f32[4,128,256]{2,1,0:T(8,128)} %copy-done.38), calls=%async_computation.1 | async-start | bytes 786432 | tf_op jit(solution)/shard_map/slice | solution.py:45
  163.3 2.6 copy-start.10
  163.3 2.6 copy-start.40
  163.3 2.6 copy-start.57
  163.3 2.6 copy-start.58
  163.3 3.9 %copy-start.59 = (f32[1,128,256]{2,1,0:T(8,128)S(1)}, f32[1,128,256]{2,1,0:T(8,128)}, u32[]{:S(2)}) copy-start(f32[1,128,256]{2,1,0:T(8,128)} %slice.961) | copy-start | bytes 393220
  163.3 5.9 %copy-start.27 = (f32[6,4,128,256]{3,2,1,0:T(8,128)S(1)}, f32[6,4,128,256]{3,2,1,0:T(8,128)}, u32[]{:S(2)}) copy-start(f32[6,4,128,256]{3,2,1,0:T(8,128)} %get-tuple-element.988) | copy-start | bytes 9437188
  163.3 5.9 %copy-start.56 = (f32[4,128,256]{2,1,0:T(8,128)S(1)}, f32[4,128,256]{2,1,0:T(8,128)}, u32[]{:S(2)}) copy-start(f32[4,128,256]{2,1,0:T(8,128)} %get-tuple-element.986) | copy-start | bytes 1572868
  165.9 1.3 copy-start.15
  167.1 12.7 %copy-start.11 = (f32[4,128,256]{2,1,0:T(8,128)S(1)}, f32[4,128,256]{2,1,0:T(8,128)}, u32[]{:S(2)}) copy-start(f32[4,128,256]{2,1,0:T(8,128)} %broadcast_multiply_fusion) | copy-start | bytes 1572868
  167.9 11.8 %collective-permute-start.7 = (f32[3,128,256]{2,1,0:T(8,128)}, f32[3,128,256]{2,1,0:T(8,128)S(1)}, u32[]{:S(2)}, u32[]{:S(2)}) collective-permute-start(f32[3,128,256]{2,1,0:T(8,128)} %pad_maximum_fusion.8), channel_id=1, source_target_pairs={{4,0},{8,4},{12,8},{16,12},{20,16},{24,20},{28,24},{32,28},{36,32}... | collective-permute-start | bytes 1179656 | tf_op jit(solution)/shard_map/ppermute | solution.py:17
  179.8 3.9 %copy-start.23 = (f32[4,128,256]{2,1,0:T(8,128)S(1)}, f32[4,128,256]{2,1,0:T(8,128)}, u32[]{:S(2)}) copy-start(f32[4,128,256]{2,1,0:T(8,128)} %get-tuple-element.888) | copy-start | bytes 1572868 | tf_op jit(solution)/shard_map/cond
  179.8 4.0 %copy-start.16 = (f32[4,128,256]{2,1,0:T(8,128)S(1)}, f32[4,128,256]{2,1,0:T(8,128)}, u32[]{:S(2)}) copy-start(f32[4,128,256]{2,1,0:T(8,128)} %get-tuple-element.884) | copy-start | bytes 1572868 | tf_op jit(solution)/shard_map/cond
  179.8 4.4 %copy-start.25 = (f32[6,4,128,256]{3,2,1,0:T(8,128)S(1)}, f32[6,4,128,256]{3,2,1,0:T(8,128)}, u32[]{:S(2)}) copy-start(f32[6,4,128,256]{3,2,1,0:T(8,128)} %get-tuple-element.1216) | copy-start | bytes 9437188 | tf_op jit(solution)/shard_map/cond
  179.8 4.4 %copy-start.35 = (f32[4,128,256]{2,1,0:T(8,128)S(1)}, f32[4,128,256]{2,1,0:T(8,128)}, u32[]{:S(2)}) copy-start(f32[4,128,256]{2,1,0:T(8,128)} %get-tuple-element.890) | copy-start | bytes 1572868 | tf_op jit(solution)/shard_map/cond
  185.1 4.2 %copy-start.36 = (f32[4,128,256]{2,1,0:T(8,128)}, f32[4,128,256]{2,1,0:T(8,128)S(1)}, u32[]{:S(2)}) copy-start(f32[4,128,256]{2,1,0:T(8,128)S(1)} %get-tuple-element.1210) | copy-start | bytes 1572868 | tf_op jit(solution)/shard_map/cond
  189.3 4.1 %copy-start.39 = (f32[4,128,256]{2,1,0:T(8,128)S(1)}, f32[4,128,256]{2,1,0:T(8,128)}, u32[]{:S(2)}) copy-start(f32[4,128,256]{2,1,0:T(8,128)} %get-tuple-element.989) | copy-start | bytes 1572868
  189.3 6.0 %copy-start.41 = (f32[4,128,256]{2,1,0:T(8,128)S(1)}, f32[4,128,256]{2,1,0:T(8,128)}, u32[]{:S(2)}) copy-start(f32[4,128,256]{2,1,0:T(8,128)} %get-tuple-element.991) | copy-start | bytes 1572868
  195.3 149.3 %copy-start.55 = (f32[4,128,256]{2,1,0:T(8,128)S(1)}, f32[4,128,256]{2,1,0:T(8,128)}, u32[]{:S(2)}) copy-start(f32[4,128,256]{2,1,0:T(8,128)} %param.22) | copy-start | bytes 1572868
  (6 other events, 5.6 us)
Sparse Core Ops, SparseCore 0:
  193.5 51.0 all-reduce.58
where the time goes:
time: 356 us; the launch traced here: 354 us
  blocking collectives  96.8 us (27%)
  other arithmetic  86.7 us (24%)
  waiting for transfers between devices  73.4 us (21%)
  local copies, waits for them, and re-layouts  49.5 us (14%)
  starting transfers between devices  30.9 us (9%)
  between operations  16.2 us (5%)
    pmax x1, blocking collectives, shards(): lax.pmax((jnp.max(jnp.abs(totals[0])), jnp.max(jnp.abs(totals[1]))), 'spa...  96.8 us
    psum x1, waiting for transfers between devices, shards(): totals = lax.psum(gradients, 'shot')  42.7 us
    ppermute x8, starting transfers between devices, shifted(): return lax.ppermute(block, axis, route)  30.8 us
    ppermute x8, waiting for transfers between devices, shifted(): return lax.ppermute(block, axis, route)  30.6 us
    scatter-add x4, other arithmetic, shards(): velocity[2] = velocity[2].reshape(-1).at[placed].add(amount).reshape(shape)  15 us
    unnamed x5, other arithmetic  9.68 us
    unnamed x91, local copies, waits for them, and re-layouts  9.49 us
    convert_element_type x1, other arithmetic, shards(): fwd = strains[step].astype(jnp.float32)  8.22 us
  transfers between devices with their start and end apart: 9, of which 8 were waited for; matrix products, arithmetic and copies ran while one was open for 14% of the time, Pallas kernels for 0%

commit v1 on v0

v1 whole, which is shorter than its diff:
```python
import jax
import jax.numpy as jnp
from jax import lax
from jax.sharding import PartitionSpec as P

STEPS = 4


COURANT = 0.15
RATE = 0.2
EPS = 1e-06


def shifted(block, axis, distance):
    devices = range(lax.axis_size(axis))
    route = [(i - distance, i) for i in devices if i - distance in devices]
    return lax.ppermute(block, axis, route)


def back_diff(field, axis):
    count = field.shape[axis]
    earlier = jnp.concatenate(
        [
            jnp.zeros_like(lax.slice_in_dim(field, 0, 1, axis=axis)),
            lax.slice_in_dim(field, 0, count - 1, axis=axis),
        ],
        axis=axis,
    )
    return field - earlier


def fore_diff(field, axis):
    count = field.shape[axis]
    later = jnp.concatenate(
        [
            lax.slice_in_dim(field, 1, count, axis=axis),
            jnp.zeros_like(lax.slice_in_dim(field, 0, 1, axis=axis)),
        ],
        axis=axis,
    )
    return later - field


def back_plane(field, plane):
    return field - jnp.concatenate([plane[None], field[:-1]], axis=0)


def fore_plane(field, plane):
    return jnp.concatenate([field[1:], plane[None]], axis=0) - field


def shards(
    adjoint_state, forward_strain, traces, receivers, sections, lame_lambda, lame_mu, buoyancy
):
    state = adjoint_state[0]
    strains = forward_strain[0]
    shot_traces = traces[0]
    shot_recv = receivers[0]
    shape = lame_lambda.shape
    cells = shape[0] * shape[1] * shape[2]
    slab = lax.axis_index("space")
    solid_flag = lax.dynamic_index_in_dim(sections, slab, keepdims=False)
    solid = solid_flag.astype(jnp.float32)
    shear = lame_mu * solid
    local = shot_recv - slab * cells
    rows = shape[0] * shape[1]
    row_hot = (lax.broadcasted_iota(jnp.int32, (rows, 256), 0) == (local >> 8)[None, :]).astype(jnp.float32)
    lane_hot = (lax.broadcasted_iota(jnp.int32, (256, shape[2]), 1) == (local & 255)[:, None]).astype(jnp.float32)
    velocity = [state[0], state[1], state[2]]
    stress = [state[3 + k] for k in range(6)]
    grad_lam = jnp.zeros(shape, jnp.float32)
    grad_shear = jnp.zeros(shape, jnp.float32)
    zero = jnp.zeros(shape[1:], jnp.float32)
    factor = COURANT * buoyancy
    factor_right = None
    for step in range(STEPS):
        amount = jnp.dot(row_hot, lane_hot * shot_traces[step][:, None], precision=lax.Precision.HIGHEST)
        part = [
            velocity[0] + factor * (back_plane(stress[0], zero) + back_diff(stress[3], 1) + back_diff(stress[4], 2)),
            velocity[1] + factor * (back_plane(stress[3], zero) + back_diff(stress[1], 1) + back_diff(stress[5], 2)),
            velocity[2] + factor * (back_plane(stress[4], zero) + back_diff(stress[5], 1) + back_diff(stress[2], 2))
            + amount.reshape(shape),
        ]
        last = [stress[0][-1], stress[3][-1], stress[4][-1]]
        left = shifted(jnp.stack(last), "space", 1)
        firsts = [p[0] for p in part]
        if step == 0:
            firsts = firsts + [factor[0]]
        right = shifted(jnp.stack(firsts), "space", -1)
        if step == 0:
            factor_right = right[3]
        velocity = [
            jnp.concatenate([(part[k][0] - factor[0] * left[k])[None], part[k][1:]], axis=0) for k in range(3)
        ]
        beyond = [right[k] - factor_right * last[k] for k in range(3)]
        fwd = strains[step].astype(jnp.float32)
        exx = fore_plane(velocity[0], beyond[0])
        eyy = fore_diff(velocity[1], 1)
        ezz = fore_diff(velocity[2], 2)
        gxy = fore_diff(velocity[0], 1) + fore_plane(velocity[1], beyond[1])
        gxz = fore_diff(velocity[0], 2) + fore_plane(velocity[2], beyond[2])
        gyz = fore_diff(velocity[1], 2) + fore_diff(velocity[2], 1)
        div = exx + eyy + ezz
        stress = [
            stress[0] + COURANT * (lame_lambda * div + 2.0 * shear * exx),
            stress[1] + COURANT * (lame_lambda * div + 2.0 * shear * eyy),
            stress[2] + COURANT * (lame_lambda * div + 2.0 * shear * ezz),
            stress[3] + COURANT * shear * gxy,
            stress[4] + COURANT * shear * gxz,
            stress[5] + COURANT * shear * gyz,
        ]
        grad_lam = grad_lam + div * (fwd[0] + fwd[1] + fwd[2])
        grad_shear = grad_shear + solid * (
            2.0 * (exx * fwd[0] + eyy * fwd[1] + ezz * fwd[2]) + gxy * fwd[3] + gxz * fwd[4] + gyz * fwd[5]
        )
    final_state = jnp.stack(velocity + stress)[None]
    return (final_state, updated_model(grad_lam, grad_shear, lame_lambda, lame_mu))


def updated_model(grad_lam, grad_shear, lame_lambda, lame_mu):
    partner = [(0, 1), (1, 0), (2, 3), (3, 2)]
    across = [(0, 2), (2, 0), (1, 3), (3, 1)]
    even = lax.axis_index("shot") % 2 == 0
    keep = jnp.where(even, grad_lam, grad_shear)
    give = jnp.where(even, grad_shear, grad_lam)
    half = keep + lax.ppermute(give, "shot", partner)
    total = half + lax.ppermute(half, "shot", across)
    other = lax.ppermute(total, "shot", partner)
    peak = jnp.max(jnp.abs(total))
    pair = jnp.stack([jnp.where(even, peak, 0.0), jnp.where(even, 0.0, peak)])
    peaks = lax.pmax(pair, ("space", "shot"))
    total_lam = jnp.where(even, total, other)
    total_mu = jnp.where(even, other, total)
    return jnp.stack(
        [
            lame_lambda * (1.0 - RATE * total_lam / (peaks[0] + EPS)),
            lame_mu * (1.0 - RATE * total_mu / (peaks[1] + EPS)),
        ]
    )


def solution(mesh):
    return jax.shard_map(
        shards,
        mesh=mesh,
        in_specs=(
            P("shot", None, "space", None, None),
            P("shot", None, None, "space", None, None),
            P("shot", None, None),
            P("shot", None),
            P(),
            P("space", None, None),
            P("space", None, None),
            P("space", None, None),
        ),
        out_specs=(P("shot", None, "space", None, None), P(None, "space", None, None)),
        check_vma=False,
    )
```

time: 356 us -> 253 us (0.71)
  local copies, waits for them, and re-layouts: 49.5 us -> 10.2 us
  other arithmetic: 86.7 us -> 65.5 us
  blocking collectives: 96.8 us -> 76.7 us
  between operations: 16.2 us -> 4.89 us
  waiting for transfers between devices: 73.4 us -> 62.2 us
    psum x1 -> x0, waiting for transfers between devices: 42.7 us -> none  [shards(): totals = lax.psum(gradients, 'shot')]
    ppermute x8, waiting for transfers between devices: 30.6 us -> 51.7 us  [shifted(): return lax.ppermute(block, axis, route)]
    pmax x1, blocking collectives: 96.8 us -> 76.7 us  [updated_model(): peaks = lax.pmax(pair, ('space', 'shot'))]
    slice x71 -> x24, local copies, waits for them, and re-layouts: 21.4 us -> 2.2 us  [the longest x10 1.21 us: shards(): last = [stress[0][-1], stress[3][-1], stress[4][-1]]]
    add x22 -> x11, other arithmetic: 28.9 us -> 12.4 us  [the longest x3 4.13 us: shards(): stress[1] + COURANT * (lame_lambda * div + 2.0 * shear * eyy)]
    scatter-add x4 -> x0, other arithmetic: 15 us -> none  [shards(): velocity[2] = velocity[2].reshape(-1).at[placed].add(amount).reshape(shape)]
    ppermute x0 -> x3, waiting for transfers between devices: none -> 10.5 us  [the longest x1 10.5 us: updated_model(): total = half + lax.ppermute(half, 'shot', across)]
    select_n x2 -> x1, other arithmetic: 1.27 us -> 10.2 us  [updated_model(): give = jnp.where(even, grad_shear, grad_lam)]
  transfers between devices with their start and end apart: 9 -> 11, of which waited for: 8 -> 8; matrix products, arithmetic and copies ran while one was open for 14% -> 18% of each run, Pallas kernels for 0% -> 0%
where the time goes in v1:
time: 253 us; the launch traced here: 252 us
  blocking collectives  76.7 us (30%)
  other arithmetic  65.5 us (26%)
  waiting for transfers between devices  62.2 us (25%)
  starting transfers between devices  29.4 us (12%)
  local copies, waits for them, and re-layouts  10.2 us (4%)
  between operations  4.89 us (2%)
  matrix products  2.75 us (1%)
    pmax x1, blocking collectives, updated_model(): peaks = lax.pmax(pair, ('space', 'shot'))  76.7 us
    ppermute x8, waiting for transfers between devices, shifted(): return lax.ppermute(block, axis, route)  51.7 us
    ppermute x8, starting transfers between devices, shifted(): return lax.ppermute(block, axis, route)  27.3 us
    ppermute x1, waiting for transfers between devices, updated_model(): total = half + lax.ppermute(half, 'shot', across)  10.5 us
    select_n x1, other arithmetic, updated_model(): give = jnp.where(even, grad_shear, grad_lam)  10.2 us
    unnamed x8, other arithmetic  9.91 us
    concatenate x22, other arithmetic, shards(): jnp.concatenate([(part[k][0] - factor[0] * left[k])[None], part[k][1:]],...  7.79 us
    convert_element_type x1, other arithmetic, shards(): fwd = strains[step].astype(jnp.float32)  6.7 us
  transfers between devices with their start and end apart: 11, of which 8 were waited for; matrix products, arithmetic and copies ran while one was open for 18% of the time, Pallas kernels for 0%

profile of v1, /device:TPU:0, one launch (start us, length us, event | category | flops | bytes accessed | tf_op | source)
XLA Modules:
  0.0 251.6 jit_solution(13146609625682135972)
XLA Ops:
  0.7 1.1 slice_bitcast_fusion.34
  1.8 0.8 pad_maximum_fusion.14
  2.6 6.7 %collective-permute-start = (f32[3,128,256]{2,1,0:T(8,128)}, f32[3,128,256]{2,1,0:T(8,128)}, u32[]{:S(2)}, u32[]{:S(2)}) collective-permute-start(f32[3,128,256]{2,1,0:T(8,128)} %pad_maximum_fusion.14), channel_id=1, source_target_pairs={{0,4},{4,8},{8,12},{12,16},{16,20},{20,24},{24,28},{28,32},{32,36}... | collective-permute-start | bytes 1179656 | tf_op jit(solution)/shard_map/ppermute | solution.py:17
  9.3 2.9 %slice_bitcast_fusion.28 = (f32[4,128,256]{2,1,0:T(8,128)S(1)}, f32[4,128,256]{2,1,0:T(8,128)S(1)}, f32[4,128,256]{2,1,0:T(8,128)}, f32[4,128,256]{2,1,0:T(8,128)}, f32[4,128,256]{2,1,0:T(8,128)}) fusion(f32[1,9,4,128,256]{4,3,2,1,0:T(8,128)} %param.8), kind=kLoop, calls=%fused_computation.236 | loop fusion | bytes 5242880 | tf_op jit(solution)/shard_map/squeeze | solution.py:70
  12.2 2.2 slice_bitcast_fusion.31
  14.5 0.5 fusion.68
  15.0 3.9 %fusion.64 = (f32[4,128,256]{2,1,0:T(8,128)S(1)}, f32[4,128,256]{2,1,0:T(8,128)S(1)}, f32[4,128,256]{2,1,0:T(8,128)}) fusion(f32[4,128,255]{2,1,0:T(8,128)} %bitcast.367, f32[4,127,256]{2,1,0:T(8,128)S(1)} %bitcast.366, f32[3,128,256]{2,1,0:T(8,128)S(1)} %get-tuple-element.50, f32[1,9,4,128,256]{4,3,2,1,0:T(8,128)} %param.8, ...), kind=kLoop, calls=%fused_computation.179 | loop fusion | flops 2097152 | bytes 9162752 | tf_op jit(solution)/shard_map/add | solution.py:79
  18.9 0.6 dynamic_slice.4
  20.2 2.1 bitcast_add_fusion.1
  22.3 0.8 copy-done.26
  23.1 1.3 fusion.67
  24.4 6.7 %slice_convert_fusion.3 = (f32[1,1,6,4,128,256]{5,4,3,2,1,0:T(8,128)S(1)}, f32[1,1,6,4,128,256]{5,4,3,2,1,0:T(8,128)S(1)}, f32[1,1,6,4,128,256]{5,4,3,2,1,0:T(8,128)}, f32[1,1,6,4,128,256]{5,4,3,2,1,0:T(8,128)}) fusion(bf16[1,4,6,4,128,256]{5,4,3,2,1,0:T(8,128)(2,1)} %param.9), kind=kLoop, calls=%fused_computation.3 | loop fusion | flops 3145728 | bytes 18874368 | tf_op jit(solution)/shard_map/convert_element_type | solution.py:96
  31.6 0.5 fusion.65
  32.1 1.2 fusion.87
  33.3 1.4 collective-permute-start.1
  35.5 14.8 %collective-permute-done.1 = f32[4,128,256]{2,1,0:T(8,128)S(1)} collective-permute-done((f32[4,128,256]{2,1,0:T(8,128)S(1)}, f32[4,128,256]{2,1,0:T(8,128)S(1)}, u32[]{:S(2)}, u32[]{:S(2)}) %collective-permute-start.1) | collective-permute-done | bytes 524320 | tf_op jit(solution)/shard_map/ppermute | solution.py:17
  50.3 1.1 slice_subtract_fusion.10
  51.4 2.6 %multiply_add_fusion.23 = (f32[4,128,256]{2,1,0:T(8,128)S(1)}, f32[4,128,256]{2,1,0:T(8,128)}, f32[4,128,256]{2,1,0:T(8,128)S(1)}, f32[4,128,256]{2,1,0:T(8,128)}) fusion(f32[1,9,4,128,256]{4,3,2,1,0:T(8,128)} %param.8, f32[4,128,256]{2,1,0:T(8,128)S(1)} %copy-done, f32[]{:T(128)} %bitcast.19, f32[3,128,256]{2,1,0:T(8,128)S(1)} %slice.782, ...), kind=kLoop, calls=%fused_computation.223 | loop fusion | flops 2228224 | bytes 6547460 | tf_op jit(solution)/shard_map/add | solution.py:108
  54.0 1.3 bitcast_add_fusion.2
  55.4 2.7 %collective-permute-start.2 = (f32[3,128,256]{2,1,0:T(8,128)S(1)}, f32[3,128,256]{2,1,0:T(8,128)S(1)}, u32[]{:S(2)}, u32[]{:S(2)}) collective-permute-start(f32[3,128,256]{2,1,0:T(8,128)S(1)} %pad_maximum_fusion.15), channel_id=1, source_target_pairs={{0,4},{4,8},{8,12},{12,16},{16,20},{20,24},{24,28},{28,32},{32,36}... | collective-permute-start | bytes 1179656 | tf_op jit(solution)/shard_map/ppermute | solution.py:17
  58.2 2.6 %multiply_add_fusion.20 = (f32[4,128,256]{2,1,0:T(8,128)S(1)}, f32[4,128,256]{2,1,0:T(8,128)S(1)}, f32[4,128,256]{2,1,0:T(8,128)S(1)}, f32[4,128,256]{2,1,0:T(8,128)}) fusion(f32[1,9,4,128,256]{4,3,2,1,0:T(8,128)} %param.8, f32[4,128,256]{2,1,0:T(8,128)S(1)} %copy-done.1, f32[4,128,256]{2,1,0:T(8,128)S(1)} %get-tuple-element.28, ...), kind=kLoop, calls=%fused_computation.220 | loop fusion | flops 2752512 | bytes 8376324 | tf_op jit(solution)/shard_map/add | solution.py:106
  60.8 0.7 multiply_add_fusion.21
  62.2 3.1 %collective-permute-done.2 = f32[3,128,256]{2,1,0:T(8,128)S(1)} collective-permute-done((f32[3,128,256]{2,1,0:T(8,128)S(1)}, f32[3,128,256]{2,1,0:T(8,128)S(1)}, u32[]{:S(2)}, u32[]{:S(2)}) %collective-permute-start.2) | collective-permute-done | bytes 393248 | tf_op jit(solution)/shard_map/ppermute | solution.py:17
  65.7 1.3 collective-permute-start.3
  67.6 11.2 %collective-permute-done.3 = f32[3,128,256]{2,1,0:T(8,128)S(1)} collective-permute-done((f32[3,128,256]{2,1,0:T(8,128)S(1)}, f32[3,128,256]{2,1,0:T(8,128)S(1)}, u32[]{:S(2)}, u32[]{:S(2)}) %collective-permute-start.3) | collective-permute-done | bytes 393248 | tf_op jit(solution)/shard_map/ppermute | solution.py:17
  78.8 1.3 multiply_add_fusion.15
  80.6 6.1 %collective-permute-start.4 = (f32[3,128,256]{2,1,0:T(8,128)S(1)}, f32[3,128,256]{2,1,0:T(8,128)S(1)}, u32[]{:S(2)}, u32[]{:S(2)}) collective-permute-start(f32[3,128,256]{2,1,0:T(8,128)S(1)} %pad_maximum_fusion.17), channel_id=1, source_target_pairs={{0,4},{4,8},{8,12},{12,16},{16,20},{20,24},{24,28},{28,32},{32,36}... | collective-permute-start | bytes 1179656 | tf_op jit(solution)/shard_map/ppermute | solution.py:17
  86.7 1.2 multiply_add_fusion.12
  87.9 0.6 multiply_add_fusion.13
  89.1 3.1 %collective-permute-done.4 = f32[3,128,256]{2,1,0:T(8,128)S(1)} collective-permute-done((f32[3,128,256]{2,1,0:T(8,128)S(1)}, f32[3,128,256]{2,1,0:T(8,128)S(1)}, u32[]{:S(2)}, u32[]{:S(2)}) %collective-permute-start.4) | collective-permute-done | bytes 393248 | tf_op jit(solution)/shard_map/ppermute | solution.py:17
  92.5 1.5 collective-permute-start.5
  94.5 9.7 %collective-permute-done.5 = f32[3,128,256]{2,1,0:T(8,128)S(1)} collective-permute-done((f32[3,128,256]{2,1,0:T(8,128)S(1)}, f32[3,128,256]{2,1,0:T(8,128)S(1)}, u32[]{:S(2)}, u32[]{:S(2)}) %collective-permute-start.5) | collective-permute-done | bytes 393248 | tf_op jit(solution)/shard_map/ppermute | solution.py:17
  105.0 1.0 multiply_add_fusion.6
  106.0 1.4 multiply_add_fusion.3
  107.4 6.3 %collective-permute-start.6 = (f32[3,128,256]{2,1,0:T(8,128)S(1)}, f32[3,128,256]{2,1,0:T(8,128)S(1)}, u32[]{:S(2)}, u32[]{:S(2)}) collective-permute-start(f32[3,128,256]{2,1,0:T(8,128)S(1)} %pad_maximum_fusion.19), channel_id=1, source_target_pairs={{0,4},{4,8},{8,12},{12,16},{16,20},{20,24},{24,28},{28,32},{32,36}... | collective-permute-start | bytes 1179656 | tf_op jit(solution)/shard_map/ppermute | solution.py:17
  113.8 0.8 add_add_fusion.1
  115.1 3.9 %collective-permute-done.6 = f32[3,128,256]{2,1,0:T(8,128)S(1)} collective-permute-done((f32[3,128,256]{2,1,0:T(8,128)S(1)}, f32[3,128,256]{2,1,0:T(8,128)S(1)}, u32[]{:S(2)}, u32[]{:S(2)}) %collective-permute-start.6) | collective-permute-done | bytes 393248 | tf_op jit(solution)/shard_map/ppermute | solution.py:17
  119.1 1.0 fusion.4
  120.1 1.0 fusion.5
  121.1 1.0 fusion.3
  122.1 0.9 fusion.2
  123.0 1.3 collective-permute-start.7
  124.3 0.8 fusion.1
  125.1 1.0 fusion
  126.2 0.8 bitcast_dynamic-update-slice_fusion.8
  127.0 0.8 bitcast_dynamic-update-slice_fusion.7
  127.8 0.8 bitcast_dynamic-update-slice_fusion.6
  128.7 6.0 %collective-permute-done.7 = f32[3,128,256]{2,1,0:T(8,128)S(1)} collective-permute-done((f32[3,128,256]{2,1,0:T(8,128)S(1)}, f32[3,128,256]{2,1,0:T(8,128)S(1)}, u32[]{:S(2)}, u32[]{:S(2)}) %collective-permute-start.7) | collective-permute-done | bytes 393248 | tf_op jit(solution)/shard_map/ppermute | solution.py:17
  134.6 0.8 slice_subtract_fusion.1
  135.4 10.2 %broadcast_select_fusion = (f32[4,128,256]{2,1,0:T(8,128)}, f32[4,128,256]{2,1,0:T(8,128)}, f32[4,128,256]{2,1,0:T(8,128)}, f32[4,128,256]{2,1,0:T(8,128)}, f32[...) fusion(pred[]{:T(512)S(6)} %eq.28, f32[1,1,6,4,128,256]{5,4,3,2,1,0:T(8,128)} %get-tuple-element.37, ...), kind=kLoop, calls=%fused_computation.259 | loop fusion | flops 14286848 | bytes 35876868 | tf_op jit(solution)/shard_map/jit(_where)/select_n | solution.py:125
  145.8 2.3 bitcast_dynamic-update-slice_fusion.5
  148.1 2.3 bitcast_dynamic-update-slice_fusion.4
  150.5 2.0 collective-permute-start.9
  152.5 1.0 bitcast_dynamic-update-slice_fusion.3
  153.5 0.9 bitcast_dynamic-update-slice_fusion.2
  154.4 10.5 %collective-permute-done.9 = f32[4,128,256]{2,1,0:T(8,128)S(1)} collective-permute-done((f32[4,128,256]{2,1,0:T(8,128)S(1)}, f32[4,128,256]{2,1,0:T(8,128)S(1)}, u32[]{:S(2)}, u32[]{:S(2)}) %collective-permute-start.9) | collective-permute-done | bytes 524320 | tf_op jit(solution)/shard_map/ppermute | solution.py:127
  164.9 0.7 abs_reduce_fusion
  165.6 0.9 bitcast_dynamic-update-slice_fusion.1
  167.9 1.9 bitcast_dynamic-update-slice_fusion
  169.8 76.7 %pmax.7 = f32[2]{0:T(128)S(1)} all-reduce(f32[2]{0:T(128)S(1)} %pad_maximum_fusion.21), channel_id=1, replica_groups=mesh['space'=32,'shot'=4] {'space','shot'}, use_global_device_ids=true, to_apply=%region_1.2 | all-reduce | flops 2 | bytes 16 | tf_op jit(solution)/shard_map/pmax | solution.py:131
  246.5 0.7 fusion.115
  248.5 0.8 copy-done.35
  249.3 1.2 multiply_bitcast_fusion.1
  250.5 1.1 pad_maximum_fusion
  (150 shorter events, 6.5 us)
Async XLA Ops:
  0.6 13.8 %copy-start.36 = (f32[1,4,256]{2,1,0:T(4,128)S(1)}, f32[1,4,256]{2,1,0:T(4,128)}, u32[]{:S(2)}) copy-start(f32[1,4,256]{2,1,0:T(4,128)} %param.10) | copy-start | bytes 12292
  0.6 13.8 %copy-start.37 = (s32[1,256]{1,0:T(1,128)S(1)}, s32[1,256]{1,0:T(1,128)}, u32[]{:S(2)}) copy-start(s32[1,256]{1,0:T(1,128)} %param.11) | copy-start | bytes 3076
  0.7 14.3 %copy-start.2 = (f32[4,128,256]{2,1,0:T(8,128)S(1)}, f32[4,128,256]{2,1,0:T(8,128)}, u32[]{:S(2)}) copy-start(f32[4,128,256]{2,1,0:T(8,128)} %param.15) | copy-start | bytes 1572868
  2.6 29.5 %collective-permute-start = (f32[3,128,256]{2,1,0:T(8,128)}, f32[3,128,256]{2,1,0:T(8,128)}, u32[]{:S(2)}, u32[]{:S(2)}) collective-permute-start(f32[3,128,256]{2,1,0:T(8,128)} %pad_maximum_fusion.14), channel_id=1, source_target_pairs={{0,4},{4,8},{8,12},{12,16},{16,20},{20,24},{24,28},{28,32},{32,36}... | collective-permute-start | bytes 1179656 | tf_op jit(solution)/shard_map/ppermute | solution.py:17
  15.0 3.9 %copy-start.38 = (s32[32]{0:T(128)S(1)}, s32[32]{0:T(128)}, u32[]{:S(2)}) copy-start(s32[32]{0:T(128)} %param.12) | copy-start | bytes 388
  22.3 0.8 copy-start.26
  24.4 7.7 %copy-start.28 = (f32[4,128,256]{2,1,0:T(8,128)S(1)}, f32[4,128,256]{2,1,0:T(8,128)}, u32[]{:S(2)}) copy-start(f32[4,128,256]{2,1,0:T(8,128)} %get-tuple-element.113) | copy-start | bytes 1572868
  33.3 27.5 %copy-start.14 = (f32[1,128,256]{2,1,0:T(8,128)}, f32[1,128,256]{2,1,0:T(8,128)S(1)}, u32[]{:S(2)}) copy-start(f32[1,128,256]{2,1,0:T(8,128)S(1)} %get-tuple-element.99) | copy-start | bytes 393220
  33.3 18.1 %copy-start = (f32[4,128,256]{2,1,0:T(8,128)S(1)}, f32[4,128,256]{2,1,0:T(8,128)}, u32[]{:S(2)}) copy-start(f32[4,128,256]{2,1,0:T(8,128)} %param.14) | copy-start | bytes 1572868
  33.3 16.9 %collective-permute-start.1 = (f32[4,128,256]{2,1,0:T(8,128)S(1)}, f32[4,128,256]{2,1,0:T(8,128)S(1)}, u32[]{:S(2)}, u32[]{:S(2)}) collective-permute-start(f32[4,128,256]{2,1,0:T(8,128)S(1)} %pad_maximum_fusion.13), channel_id=1, source_target_pairs={{4,0},{8,4},{12,8},{16,12},{20,16},{24,20},{28,24},{32,28},{36,32}... | collective-permute-start | bytes 1572872 | tf_op jit(solution)/shard_map/ppermute | solution.py:17
  35.1 23.1 %copy-start.7 = (f32[4,127,256]{2,1,0:T(8,128)}, f32[4,127,256]{2,1,0:T(8,128)S(1)}, u32[]{:S(2)}) copy-start(f32[4,127,256]{2,1,0:T(8,128)S(1)} %get-tuple-element.125) | copy-start | bytes 1560580
  35.5 26.0 %copy-start.9 = (f32[4,128,255]{2,1,0:T(8,128)}, f32[4,128,255]{2,1,0:T(8,128)S(1)}, u32[]{:S(2)}) copy-start(f32[4,128,255]{2,1,0:T(8,128)S(1)} %get-tuple-element.122) | copy-start | bytes 1566724
  35.5 18.5 %copy-start.1 = (f32[4,128,256]{2,1,0:T(8,128)S(1)}, f32[4,128,256]{2,1,0:T(8,128)}, u32[]{:S(2)}) copy-start(f32[4,128,256]{2,1,0:T(8,128)} %param.13) | copy-start | bytes 1572868
  51.3 4.0 %copy-start.33 = (f32[1,128,256]{2,1,0:T(8,128)}, f32[1,128,256]{2,1,0:T(8,128)S(1)}, u32[]{:S(2)}) copy-start(f32[1,128,256]{2,1,0:T(8,128)S(1)} %get-tuple-element.47) | copy-start | bytes 393220
  55.3 5.5 %copy-start.21 = (f32[4,128,256]{2,1,0:T(8,128)}, f32[4,128,256]{2,1,0:T(8,128)S(1)}, u32[]{:S(2)}) copy-start(f32[4,128,256]{2,1,0:T(8,128)S(1)} %get-tuple-element.28) | copy-start | bytes 1572868
  55.4 9.9 %collective-permute-start.2 = (f32[3,128,256]{2,1,0:T(8,128)S(1)}, f32[3,128,256]{2,1,0:T(8,128)S(1)}, u32[]{:S(2)}, u32[]{:S(2)}) collective-permute-start(f32[3,128,256]{2,1,0:T(8,128)S(1)} %pad_maximum_fusion.15), channel_id=1, source_target_pairs={{0,4},{4,8},{8,12},{12,16},{16,20},{20,24},{24,28},{28,32},{32,36}... | collective-permute-start | bytes 1179656 | tf_op jit(solution)/shard_map/ppermute | solution.py:17
  60.8 1.0 copy-start.27
  65.4 22.5 %copy-start.15 = (f32[1,128,256]{2,1,0:T(8,128)}, f32[1,128,256]{2,1,0:T(8,128)S(1)}, u32[]{:S(2)}) copy-start(f32[1,128,256]{2,1,0:T(8,128)S(1)} %get-tuple-element.96) | copy-start | bytes 393220
  65.7 13.0 %collective-permute-start.3 = (f32[3,128,256]{2,1,0:T(8,128)S(1)}, f32[3,128,256]{2,1,0:T(8,128)S(1)}, u32[]{:S(2)}, u32[]{:S(2)}) collective-permute-start(f32[3,128,256]{2,1,0:T(8,128)S(1)} %pad_maximum_fusion.16), channel_id=1, source_target_pairs={{4,0},{8,4},{12,8},{16,12},{20,16},{24,20},{28,24},{32,28},{36,32}... | collective-permute-start | bytes 1179656 | tf_op jit(solution)/shard_map/ppermute | solution.py:17
  67.3 19.4 %copy-start.10 = (f32[4,127,256]{2,1,0:T(8,128)}, f32[4,127,256]{2,1,0:T(8,128)S(1)}, u32[]{:S(2)}) copy-start(f32[4,127,256]{2,1,0:T(8,128)S(1)} %fusion.14) | copy-start | bytes 1560580
  67.5 19.1 %copy-start.11 = (f32[4,128,255]{2,1,0:T(8,128)}, f32[4,128,255]{2,1,0:T(8,128)S(1)}, u32[]{:S(2)}) copy-start(f32[4,128,255]{2,1,0:T(8,128)S(1)} %fusion.12) | copy-start | bytes 1566724
  78.8 1.7 copy-start.34
  80.5 7.5 %copy-start.22 = (f32[4,128,256]{2,1,0:T(8,128)}, f32[4,128,256]{2,1,0:T(8,128)S(1)}, u32[]{:S(2)}) copy-start(f32[4,128,256]{2,1,0:T(8,128)S(1)} %get-tuple-element.20) | copy-start | bytes 1572868
  80.6 11.6 %collective-permute-start.4 = (f32[3,128,256]{2,1,0:T(8,128)S(1)}, f32[3,128,256]{2,1,0:T(8,128)S(1)}, u32[]{:S(2)}, u32[]{:S(2)}) collective-permute-start(f32[3,128,256]{2,1,0:T(8,128)S(1)} %pad_maximum_fusion.17), channel_id=1, source_target_pairs={{0,4},{4,8},{8,12},{12,16},{16,20},{20,24},{24,28},{28,32},{32,36}... | collective-permute-start | bytes 1179656 | tf_op jit(solution)/shard_map/ppermute | solution.py:17
  92.3 12.3 %copy-start.13 = (f32[4,127,256]{2,1,0:T(8,128)}, f32[4,127,256]{2,1,0:T(8,128)S(1)}, u32[]{:S(2)}) copy-start(f32[4,127,256]{2,1,0:T(8,128)S(1)} %fusion.8) | copy-start | bytes 1560580
  92.5 11.6 %collective-permute-start.5 = (f32[3,128,256]{2,1,0:T(8,128)S(1)}, f32[3,128,256]{2,1,0:T(8,128)S(1)}, u32[]{:S(2)}, u32[]{:S(2)}) collective-permute-start(f32[3,128,256]{2,1,0:T(8,128)S(1)} %pad_maximum_fusion.18), channel_id=1, source_target_pairs={{4,0},{8,4},{12,8},{16,12},{20,16},{24,20},{28,24},{32,28},{36,32}... | collective-permute-start | bytes 1179656 | tf_op jit(solution)/shard_map/ppermute | solution.py:17
  94.2 10.3 %copy-start.23 = (f32[4,128,255]{2,1,0:T(8,128)}, f32[4,128,255]{2,1,0:T(8,128)S(1)}, u32[]{:S(2)}) copy-start(f32[4,128,255]{2,1,0:T(8,128)S(1)} %fusion.6) | copy-start | bytes 1566724
  104.2 0.6 copy-start.25
  104.6 1.4 copy-start.24
  104.6 9.2 %copy-start.3 = (f32[4,128,256]{2,1,0:T(8,128)}, f32[4,128,256]{2,1,0:T(8,128)S(1)}, u32[]{:S(2)}) copy-start(f32[4,128,256]{2,1,0:T(8,128)S(1)} %get-tuple-element.11) | copy-start | bytes 1572868
  104.9 9.7 %copy-start.5 = (f32[4,128,256]{2,1,0:T(8,128)}, f32[4,128,256]{2,1,0:T(8,128)S(1)}, u32[]{:S(2)}) copy-start(f32[4,128,256]{2,1,0:T(8,128)S(1)} %get-tuple-element.61) | copy-start | bytes 1572868
  107.4 11.6 %collective-permute-start.6 = (f32[3,128,256]{2,1,0:T(8,128)S(1)}, f32[3,128,256]{2,1,0:T(8,128)S(1)}, u32[]{:S(2)}, u32[]{:S(2)}) collective-permute-start(f32[3,128,256]{2,1,0:T(8,128)S(1)} %pad_maximum_fusion.19), channel_id=1, source_target_pairs={{0,4},{4,8},{8,12},{12,16},{16,20},{20,24},{24,28},{28,32},{32,36}... | collective-permute-start | bytes 1179656 | tf_op jit(solution)/shard_map/ppermute | solution.py:17
  119.1 9.6 %copy-start.16 = (f32[1,128,256]{2,1,0:T(8,128)}, f32[1,128,256]{2,1,0:T(8,128)S(1)}, u32[]{:S(2)}) copy-start(f32[1,128,256]{2,1,0:T(8,128)S(1)} %get-tuple-element.82) | copy-start | bytes 393220
  119.1 9.6 %copy-start.18 = (f32[1,128,256]{2,1,0:T(8,128)}, f32[1,128,256]{2,1,0:T(8,128)S(1)}, u32[]{:S(2)}) copy-start(f32[1,128,256]{2,1,0:T(8,128)S(1)} %get-tuple-element.83) | copy-start | bytes 393220
  119.1 9.6 %copy-start.19 = (f32[1,128,256]{2,1,0:T(8,128)}, f32[1,128,256]{2,1,0:T(8,128)S(1)}, u32[]{:S(2)}) copy-start(f32[1,128,256]{2,1,0:T(8,128)S(1)} %get-tuple-element.84) | copy-start | bytes 393220
  121.1 14.3 %copy-start.8 = (f32[4,127,256]{2,1,0:T(8,128)S(1)}, f32[4,127,256]{2,1,0:T(8,128)}, u32[]{:S(2)}) copy-start(f32[4,127,256]{2,1,0:T(8,128)} %copy-done.7) | copy-start | bytes 1560580
  123.0 11.6 %collective-permute-start.7 = (f32[3,128,256]{2,1,0:T(8,128)S(1)}, f32[3,128,256]{2,1,0:T(8,128)S(1)}, u32[]{:S(2)}, u32[]{:S(2)}) collective-permute-start(f32[3,128,256]{2,1,0:T(8,128)S(1)} %pad_maximum_fusion.20), channel_id=1, source_target_pairs={{4,0},{8,4},{12,8},{16,12},{20,16},{24,20},{28,24},{32,28},{36,32}... | collective-permute-start | bytes 1179656 | tf_op jit(solution)/shard_map/ppermute | solution.py:17
  135.4 12.7 %copy-start.6 = (f32[4,128,256]{2,1,0:T(8,128)S(1)}, f32[4,128,256]{2,1,0:T(8,128)}, u32[]{:S(2)}) copy-start(f32[4,128,256]{2,1,0:T(8,128)} %copy-done.5) | copy-start | bytes 1572868
  145.6 4.8 %copy-start.31 = (f32[4,128,256]{2,1,0:T(8,128)S(1)}, f32[4,128,256]{2,1,0:T(8,128)}, u32[]{:S(2)}) copy-start(f32[4,128,256]{2,1,0:T(8,128)} %get-tuple-element.5) | copy-start | bytes 1572868
  145.6 4.8 %copy-start.32 = (f32[4,128,256]{2,1,0:T(8,128)S(1)}, f32[4,128,256]{2,1,0:T(8,128)}, u32[]{:S(2)}) copy-start(f32[4,128,256]{2,1,0:T(8,128)} %get-tuple-element.6) | copy-start | bytes 1572868
  145.7 6.9 %copy-start.4 = (f32[4,128,256]{2,1,0:T(8,128)S(1)}, f32[4,128,256]{2,1,0:T(8,128)}, u32[]{:S(2)}) copy-start(f32[4,128,256]{2,1,0:T(8,128)} %copy-done.3) | copy-start | bytes 1572868
  145.7 6.8 %copy-start.12 = (f32[4,128,256]{2,1,0:T(8,128)S(1)}, f32[4,128,256]{2,1,0:T(8,128)}, u32[]{:S(2)}) copy-start(f32[4,128,256]{2,1,0:T(8,128)} %get-tuple-element.10) | copy-start | bytes 1572868
  145.7 6.8 %copy-start.17 = (f32[1,128,256]{2,1,0:T(8,128)S(1)}, f32[1,128,256]{2,1,0:T(8,128)}, u32[]{:S(2)}) copy-start(f32[1,128,256]{2,1,0:T(8,128)} %copy-done.16) | copy-start | bytes 393220
  145.7 6.8 %copy-start.20 = (f32[4,128,255]{2,1,0:T(8,128)S(1)}, f32[4,128,255]{2,1,0:T(8,128)}, u32[]{:S(2)}) copy-start(f32[4,128,255]{2,1,0:T(8,128)} %fusion) | copy-start | bytes 1566724
  145.7 4.7 %collective-permute-start.8 = (f32[4,128,256]{2,1,0:T(8,128)}, f32[4,128,256]{2,1,0:T(8,128)S(1)}, u32[]{:S(2)}, u32[]{:S(2)}) collective-permute-start(f32[4,128,256]{2,1,0:T(8,128)} %get-tuple-element.4), channel_id=1, source_target_pairs={{0,1},{1,0},{2,3},{3,2},{4,5},{5,4},{6,7},{7,6},{8,9},{9,8},{10,11... | collective-permute-start | bytes 1572872 | tf_op jit(solution)/shard_map/ppermute | solution.py:126
  148.1 5.4 %copy-start.30 = (f32[4,128,256]{2,1,0:T(8,128)S(1)}, f32[4,128,256]{2,1,0:T(8,128)}, u32[]{:S(2)}) copy-start(f32[4,128,256]{2,1,0:T(8,128)} %get-tuple-element.9) | copy-start | bytes 1572868
  150.4 15.2 %copy-start.29 = (f32[4,128,256]{2,1,0:T(8,128)S(1)}, f32[4,128,256]{2,1,0:T(8,128)}, u32[]{:S(2)}) copy-start(f32[4,128,256]{2,1,0:T(8,128)} %get-tuple-element.8) | copy-start | bytes 1572868
  150.5 14.4 %collective-permute-start.9 = (f32[4,128,256]{2,1,0:T(8,128)S(1)}, f32[4,128,256]{2,1,0:T(8,128)S(1)}, u32[]{:S(2)}, u32[]{:S(2)}) collective-permute-start(f32[4,128,256]{2,1,0:T(8,128)S(1)} %select_add_fusion), channel_id=1, source_target_pairs={{0,2},{2,0},{1,3},{3,1},{4,6},{6,4},{5,7},{7,5},{8,10},{10,8},{9,1... | collective-permute-start | bytes 1572872 | tf_op jit(solution)/shard_map/ppermute | solution.py:127
  165.6 82.9 %collective-permute-start.10 = (f32[4,128,256]{2,1,0:T(8,128)S(1)}, f32[4,128,256]{2,1,0:T(8,128)S(1)}, u32[]{:S(2)}, u32[]{:S(2)}) collective-permute-start(f32[4,128,256]{2,1,0:T(8,128)S(1)} %get-tuple-element.3), channel_id=1, source_target_pairs={{0,1},{1,0},{2,3},{3,2},{4,5},{5,4},{6,7},{7,6},{8,9},{9,8},{10,11... | collective-permute-start | bytes 1572872 | tf_op jit(solution)/shard_map/ppermute | solution.py:128
  248.5 0.8 copy-start.35

commit v2 on v1

--- a/solution.py
+++ b/solution.py
@@ -117,6 +117,19 @@
     return (final_state, updated_model(grad_lam, grad_shear, lame_lambda, lame_mu))
 
 
+def space_peak(value):
+    count = lax.axis_size("space")
+    for stride, size in ((2, 4), (8, 4), (1, 2)):
+        span = stride * size
+        arrived = []
+        for turn in range(1, size):
+            route = [(i, i // span * span + (i + turn * stride) % span) for i in range(count)]
+            arrived.append(lax.ppermute(value, "space", route))
+        for item in arrived:
+            value = jnp.maximum(value, item)
+    return value
+
+
 def updated_model(grad_lam, grad_shear, lame_lambda, lame_mu):
     partner = [(0, 1), (1, 0), (2, 3), (3, 2)]
     across = [(0, 2), (2, 0), (1, 3), (3, 1)]
@@ -127,8 +140,9 @@
     total = half + lax.ppermute(half, "shot", across)
     other = lax.ppermute(total, "shot", partner)
     peak = jnp.max(jnp.abs(total))
-    pair = jnp.stack([jnp.where(even, peak, 0.0), jnp.where(even, 0.0, peak)])
-    peaks = lax.pmax(pair, ("space", "shot"))
+    own = space_peak(jnp.full((8, 128), peak))
+    theirs = lax.ppermute(own, "shot", partner)
+    peaks = (jnp.where(even, own, theirs)[0, 0], jnp.where(even, theirs, own)[0, 0])
     total_lam = jnp.where(even, total, other)
     total_mu = jnp.where(even, other, total)
     return jnp.stack(

time: 253 us -> 199 us (0.79)
  blocking collectives: 76.7 us -> 0 us
  starting transfers between devices: 29.4 us -> 51.6 us
  other arithmetic: 65.5 us -> 53.6 us
  waiting for transfers between devices: 62.2 us -> 73.9 us
    pmax x1 -> x0, blocking collectives: 76.7 us -> none  [updated_model(): peaks = lax.pmax(pair, ('space', 'shot'))]
    ppermute x0 -> x8, starting transfers between devices: none -> 22.1 us  [the longest x7 22.1 us: space_peak(): arrived.append(lax.ppermute(value, 'space', route))]
    ppermute x0 -> x8, waiting for transfers between devices: none -> 8.27 us  [the longest x7 7.23 us: space_peak(): arrived.append(lax.ppermute(value, 'space', route))]
    unnamed x8 -> x9, other arithmetic: 9.91 us -> 3.76 us
  transfers between devices with their start and end apart: 11 -> 19, of which waited for: 8 -> 14; matrix products, arithmetic and copies ran while one was open for 18% -> 20% of each run, Pallas kernels for 0% -> 0%
where the time goes in v2:
time: 199 us; the launch traced here: 198 us
  waiting for transfers between devices  73.9 us (37%)
  other arithmetic  53.6 us (27%)
  starting transfers between devices  51.6 us (26%)
  local copies, waits for them, and re-layouts  12.2 us (6%)
  between operations  3.62 us (2%)
  matrix products  2.77 us (1%)
    ppermute x8, waiting for transfers between devices, shifted(): return lax.ppermute(block, axis, route)  53.6 us
    ppermute x8, starting transfers between devices, shifted(): return lax.ppermute(block, axis, route)  27.3 us
    ppermute x7, starting transfers between devices, space_peak(): arrived.append(lax.ppermute(value, 'space', route))  22.1 us
    ppermute x1, waiting for transfers between devices, updated_model(): total = half + lax.ppermute(half, 'shot', across)  12 us
    select_n x1, other arithmetic, updated_model(): give = jnp.where(even, grad_shear, grad_lam)  10.2 us
    concatenate x22, other arithmetic, shards(): jnp.concatenate([(part[k][0] - factor[0] * left[k])[None], part[k][1:]],...  7.83 us
    ppermute x7, waiting for transfers between devices, space_peak(): arrived.append(lax.ppermute(value, 'space', route))  7.23 us
    convert_element_type x1, other arithmetic, shards(): fwd = strains[step].astype(jnp.float32)  7.09 us
  transfers between devices with their start and end apart: 19, of which 14 were waited for; matrix products, arithmetic and copies ran while one was open for 20% of the time, Pallas kernels for 0%

profile of v2, /device:TPU:0, one launch (start us, length us, event | category | flops | bytes accessed | tf_op | source)
XLA Modules:
  0.0 197.6 jit_solution(8130012604495318597)
XLA Ops:
  0.7 1.1 slice_bitcast_fusion.34
  1.8 0.8 pad_maximum_fusion.14
  2.6 6.7 %collective-permute-start = (f32[3,128,256]{2,1,0:T(8,128)}, f32[3,128,256]{2,1,0:T(8,128)}, u32[]{:S(2)}, u32[]{:S(2)}) collective-permute-start(f32[3,128,256]{2,1,0:T(8,128)} %pad_maximum_fusion.14), channel_id=1, source_target_pairs={{0,4},{4,8},{8,12},{12,16},{16,20},{20,24},{24,28},{28,32},{32,36}... | collective-permute-start | bytes 1179656 | tf_op jit(solution)/shard_map/ppermute | solution.py:17
  9.3 2.9 %slice_bitcast_fusion.28 = (f32[4,128,256]{2,1,0:T(8,128)S(1)}, f32[4,128,256]{2,1,0:T(8,128)S(1)}, f32[4,128,256]{2,1,0:T(8,128)}, f32[4,128,256]{2,1,0:T(8,128)S(1)}, f32[4,128,256]{2,1,0:T(8,128)}) fusion(f32[1,9,4,128,256]{4,3,2,1,0:T(8,128)} %param.8), kind=kLoop, calls=%fused_computation.236 | loop fusion | bytes 5242880 | tf_op jit(solution)/shard_map/squeeze | solution.py:70
  12.1 2.2 %slice_bitcast_fusion.31 = (f32[3,128,256]{2,1,0:T(8,128)S(1)}, f32[3,128,256]{2,1,0:T(8,128)}, f32[3,128,256]{2,1,0:T(8,128)}) fusion(f32[1,9,4,128,256]{4,3,2,1,0:T(8,128)} %param.8), kind=kLoop, calls=%fused_computation.248 | loop fusion | bytes 2359296 | tf_op jit(solution)/shard_map/slice | solution.py:45
  15.4 3.8 %fusion.64 = (f32[4,128,256]{2,1,0:T(8,128)S(1)}, f32[4,128,256]{2,1,0:T(8,128)S(1)}, f32[4,128,256]{2,1,0:T(8,128)}) fusion(f32[4,128,255]{2,1,0:T(8,128)S(1)} %bitcast.367, f32[4,127,256]{2,1,0:T(8,128)S(1)} %bitcast.366, f32[3,128,256]{2,1,0:T(8,128)S(1)} %get-tuple-element.50, f32[1,9,4,128,256]{4,3,2,1,0:T(8,128)} %param.8, ...), kind=kLoop, calls=%fused_computation.179 | loop fusion | flops 2097152 | bytes 9162752 | tf_op jit(solution)/shard_map/add | solution.py:79
  19.2 1.2 dynamic_slice.4
  21.1 2.1 %bitcast_add_fusion.1 = f32[4,128,256]{2,1,0:T(8,128)S(1)} fusion(f32[4,128,255]{2,1,0:T(8,128)S(1)} %bitcast.364, f32[4,127,256]{2,1,0:T(8,128)} %bitcast.365, f32[3,128,256]{2,1,0:T(8,128)} %get-tuple-element.51, f32[1,9,4,128,256]{4,3,2,1,0:T(8,128)} %param.8, f32[4,128,256]{2,1,0:T(8,128)S(1)} %copy-done.2), kind=kLoop, calls=%fused_computation.173 | loop fusion | flops 1048576 | bytes 4581376 | tf_op jit(solution)/shard_map/add | solution.py:80
  23.3 0.8 copy-done.28
  24.1 1.3 fusion.67
  25.4 7.1 %slice_convert_fusion.3 = (f32[1,1,6,4,128,256]{5,4,3,2,1,0:T(8,128)S(1)}, f32[1,1,6,4,128,256]{5,4,3,2,1,0:T(8,128)}, f32[1,1,6,4,128,256]{5,4,3,2,1,0:T(8,128)}, f32[1,1,6,4,128,256]{5,4,3,2,1,0:T(8,128)}) fusion(bf16[1,4,6,4,128,256]{5,4,3,2,1,0:T(8,128)(2,1)} %param.9), kind=kLoop, calls=%fused_computation.3 | loop fusion | flops 3145728 | bytes 18874368 | tf_op jit(solution)/shard_map/convert_element_type | solution.py:96
  33.5 1.2 fusion.87
  34.7 1.4 collective-permute-start.1
  36.9 14.8 %collective-permute-done.1 = f32[4,128,256]{2,1,0:T(8,128)S(1)} collective-permute-done((f32[4,128,256]{2,1,0:T(8,128)S(1)}, f32[4,128,256]{2,1,0:T(8,128)S(1)}, u32[]{:S(2)}, u32[]{:S(2)}) %collective-permute-start.1) | collective-permute-done | bytes 524320 | tf_op jit(solution)/shard_map/ppermute | solution.py:17
  51.7 1.3 multiply_add_fusion.23
  53.5 2.7 %collective-permute-start.2 = (f32[3,128,256]{2,1,0:T(8,128)S(1)}, f32[3,128,256]{2,1,0:T(8,128)S(1)}, u32[]{:S(2)}, u32[]{:S(2)}) collective-permute-start(f32[3,128,256]{2,1,0:T(8,128)S(1)} %pad_maximum_fusion.15), channel_id=1, source_target_pairs={{0,4},{4,8},{8,12},{12,16},{16,20},{20,24},{24,28},{28,32},{32,36}... | collective-permute-start | bytes 1179656 | tf_op jit(solution)/shard_map/ppermute | solution.py:17
  56.2 1.3 multiply_add_fusion.20
  59.0 4.4 %collective-permute-done.2 = f32[3,128,256]{2,1,0:T(8,128)S(1)} collective-permute-done((f32[3,128,256]{2,1,0:T(8,128)S(1)}, f32[3,128,256]{2,1,0:T(8,128)S(1)}, u32[]{:S(2)}, u32[]{:S(2)}) %collective-permute-start.2) | collective-permute-done | bytes 393248 | tf_op jit(solution)/shard_map/ppermute | solution.py:17
  63.8 1.3 collective-permute-start.3
  65.6 11.2 %collective-permute-done.3 = f32[3,128,256]{2,1,0:T(8,128)S(1)} collective-permute-done((f32[3,128,256]{2,1,0:T(8,128)S(1)}, f32[3,128,256]{2,1,0:T(8,128)S(1)}, u32[]{:S(2)}, u32[]{:S(2)}) %collective-permute-start.3) | collective-permute-done | bytes 393248 | tf_op jit(solution)/shard_map/ppermute | solution.py:17
  76.9 1.3 multiply_add_fusion.15
  78.6 6.1 %collective-permute-start.4 = (f32[3,128,256]{2,1,0:T(8,128)S(1)}, f32[3,128,256]{2,1,0:T(8,128)S(1)}, u32[]{:S(2)}, u32[]{:S(2)}) collective-permute-start(f32[3,128,256]{2,1,0:T(8,128)S(1)} %pad_maximum_fusion.17), channel_id=1, source_target_pairs={{0,4},{4,8},{8,12},{12,16},{16,20},{20,24},{24,28},{28,32},{32,36}... | collective-permute-start | bytes 1179656 | tf_op jit(solution)/shard_map/ppermute | solution.py:17
  84.7 1.2 multiply_add_fusion.12
  87.1 3.0 %collective-permute-done.4 = f32[3,128,256]{2,1,0:T(8,128)S(1)} collective-permute-done((f32[3,128,256]{2,1,0:T(8,128)S(1)}, f32[3,128,256]{2,1,0:T(8,128)S(1)}, u32[]{:S(2)}, u32[]{:S(2)}) %collective-permute-start.4) | collective-permute-done | bytes 393248 | tf_op jit(solution)/shard_map/ppermute | solution.py:17
  90.6 1.5 collective-permute-start.5
  92.5 9.7 %collective-permute-done.5 = f32[3,128,256]{2,1,0:T(8,128)S(1)} collective-permute-done((f32[3,128,256]{2,1,0:T(8,128)S(1)}, f32[3,128,256]{2,1,0:T(8,128)S(1)}, u32[]{:S(2)}, u32[]{:S(2)}) %collective-permute-start.5) | collective-permute-done | bytes 393248 | tf_op jit(solution)/shard_map/ppermute | solution.py:17
  103.0 1.0 multiply_add_fusion.6
  104.0 1.3 multiply_add_fusion.3
  105.4 6.3 %collective-permute-start.6 = (f32[3,128,256]{2,1,0:T(8,128)S(1)}, f32[3,128,256]{2,1,0:T(8,128)S(1)}, u32[]{:S(2)}, u32[]{:S(2)}) collective-permute-start(f32[3,128,256]{2,1,0:T(8,128)S(1)} %pad_maximum_fusion.19), channel_id=1, source_target_pairs={{0,4},{4,8},{8,12},{12,16},{16,20},{20,24},{24,28},{28,32},{32,36}... | collective-permute-start | bytes 1179656 | tf_op jit(solution)/shard_map/ppermute | solution.py:17
  111.7 0.7 add_add_fusion.1
  113.0 4.0 %collective-permute-done.6 = f32[3,128,256]{2,1,0:T(8,128)S(1)} collective-permute-done((f32[3,128,256]{2,1,0:T(8,128)S(1)}, f32[3,128,256]{2,1,0:T(8,128)S(1)}, u32[]{:S(2)}, u32[]{:S(2)}) %collective-permute-start.6) | collective-permute-done | bytes 393248 | tf_op jit(solution)/shard_map/ppermute | solution.py:17
  117.1 0.9 fusion.4
  118.0 1.0 fusion.5
  119.0 1.3 collective-permute-start.7
  120.3 1.0 fusion.3
  121.4 0.9 fusion.2
  122.3 0.8 fusion.1
  123.1 1.1 fusion
  124.2 6.5 %collective-permute-done.7 = f32[3,128,256]{2,1,0:T(8,128)S(1)} collective-permute-done((f32[3,128,256]{2,1,0:T(8,128)S(1)}, f32[3,128,256]{2,1,0:T(8,128)S(1)}, u32[]{:S(2)}, u32[]{:S(2)}) %collective-permute-start.7) | collective-permute-done | bytes 393248 | tf_op jit(solution)/shard_map/ppermute | solution.py:17
  130.7 0.8 slice_subtract_fusion.1
  131.5 10.2 %broadcast_select_fusion = (f32[4,128,256]{2,1,0:T(8,128)}, f32[4,128,256]{2,1,0:T(8,128)}, f32[4,128,256]{2,1,0:T(8,128)}, f32[4,128,256]{2,1,0:T(8,128)}, f32[...) fusion(pred[]{:T(512)S(6)} %eq.28, f32[1,1,6,4,128,256]{5,4,3,2,1,0:T(8,128)} %get-tuple-element.37, ...), kind=kLoop, calls=%fused_computation.259 | loop fusion | flops 14286848 | bytes 35876868 | tf_op jit(solution)/shard_map/jit(_where)/select_n | solution.py:138
  141.9 1.1 bitcast_dynamic-update-slice_fusion.8
  142.9 0.9 bitcast_dynamic-update-slice_fusion.7
  143.9 0.9 bitcast_dynamic-update-slice_fusion.6
  144.8 1.2 select_add_fusion
  146.0 2.0 %collective-permute-start.9 = (f32[4,128,256]{2,1,0:T(8,128)S(1)}, f32[4,128,256]{2,1,0:T(8,128)S(1)}, u32[]{:S(2)}, u32[]{:S(2)}) collective-permute-start(f32[4,128,256]{2,1,0:T(8,128)S(1)} %select_add_fusion), channel_id=1, source_target_pairs={{0,2},{2,0},{1,3},{3,1},{4,6},{6,4},{5,7},{7,5},{8,10},{10,8},{9,1... | collective-permute-start | bytes 1572872 | tf_op jit(solution)/shard_map/ppermute | solution.py:140
  148.5 12.0 %collective-permute-done.9 = f32[4,128,256]{2,1,0:T(8,128)S(1)} collective-permute-done((f32[4,128,256]{2,1,0:T(8,128)S(1)}, f32[4,128,256]{2,1,0:T(8,128)S(1)}, u32[]{:S(2)}, u32[]{:S(2)}) %collective-permute-start.9) | collective-permute-done | bytes 524320 | tf_op jit(solution)/shard_map/ppermute | solution.py:140
  160.5 0.7 abs_reduce_fusion
  161.1 0.6 broadcast_in_dim.5
  161.8 4.3 %collective-permute-start.11 = (f32[8,128]{1,0:T(8,128)S(1)}, f32[8,128]{1,0:T(8,128)S(1)}, u32[]{:S(2)}, u32[]{:S(2)}) collective-permute-start(f32[8,128]{1,0:T(8,128)S(1)} %broadcast_in_dim.5), channel_id=1, source_target_pairs={{0,8},{4,12},{8,16},{12,20},{16,24},{20,28},{24,0},{28,4},{32,40},... | collective-permute-start | bytes 12296 | tf_op jit(solution)/shard_map/ppermute | solution.py:127
  166.1 6.2 %collective-permute-start.12 = (f32[8,128]{1,0:T(8,128)S(1)}, f32[8,128]{1,0:T(8,128)S(1)}, u32[]{:S(2)}, u32[]{:S(2)}) collective-permute-start(f32[8,128]{1,0:T(8,128)S(1)} %broadcast_in_dim.5), channel_id=1, source_target_pairs={{0,16},{4,20},{8,24},{12,28},{16,0},{20,4},{24,8},{28,12},{32,48},... | collective-permute-start | bytes 12296 | tf_op jit(solution)/shard_map/ppermute | solution.py:127
  172.5 1.4 collective-permute-done.12
  173.9 2.0 %collective-permute-done.13 = f32[8,128]{1,0:T(8,128)S(1)} collective-permute-done((f32[8,128]{1,0:T(8,128)S(1)}, f32[8,128]{1,0:T(8,128)S(1)}, u32[]{:S(2)}, u32[]{:S(2)}) %collective-permute-start.13) | collective-permute-done | bytes 4128 | tf_op jit(solution)/shard_map/ppermute | solution.py:127
  175.9 0.6 maximum_maximum_fusion.1
  176.5 2.4 %collective-permute-start.14 = (f32[8,128]{1,0:T(8,128)S(1)}, f32[8,128]{1,0:T(8,128)S(1)}, u32[]{:S(2)}, u32[]{:S(2)}) collective-permute-start(f32[8,128]{1,0:T(8,128)S(1)} %maximum_maximum_fusion.1), channel_id=1, source_target_pairs={{0,32},{4,36},{8,40},{12,44},{16,48},{20,52},{24,56},{28,60},{32,6... | collective-permute-start | bytes 12296 | tf_op jit(solution)/shard_map/ppermute | solution.py:127
  178.9 3.2 %collective-permute-start.15 = (f32[8,128]{1,0:T(8,128)S(1)}, f32[8,128]{1,0:T(8,128)S(1)}, u32[]{:S(2)}, u32[]{:S(2)}) collective-permute-start(f32[8,128]{1,0:T(8,128)S(1)} %maximum_maximum_fusion.1), channel_id=1, source_target_pairs={{0,64},{4,68},{8,72},{12,76},{16,80},{20,84},{24,88},{28,92},{32,9... | collective-permute-start | bytes 12296 | tf_op jit(solution)/shard_map/ppermute | solution.py:127
  182.1 1.0 collective-permute-start.16
  183.3 0.7 collective-permute-done.15
  184.1 1.7 collective-permute-done.16
  185.7 5.1 %collective-permute-start.17 = (f32[8,128]{1,0:T(8,128)S(1)}, f32[8,128]{1,0:T(8,128)S(1)}, u32[]{:S(2)}, u32[]{:S(2)}) collective-permute-start(f32[8,128]{1,0:T(8,128)S(1)} %maximum_maximum_fusion), channel_id=1, source_target_pairs={{0,4},{4,0},{8,12},{12,8},{16,20},{20,16},{24,28},{28,24},{32,36},... | collective-permute-start | bytes 12296 | tf_op jit(solution)/shard_map/ppermute | solution.py:127
  190.9 1.5 collective-permute-done.17
  192.5 1.0 collective-permute-done.18
  193.5 1.0 slice.765
  196.5 1.1 pad_maximum_fusion
  (179 shorter events, 11.2 us)
Async XLA Ops:
  0.6 13.7 %copy-start.39 = (f32[1,4,256]{2,1,0:T(4,128)S(1)}, f32[1,4,256]{2,1,0:T(4,128)}, u32[]{:S(2)}) copy-start(f32[1,4,256]{2,1,0:T(4,128)} %param.10) | copy-start | bytes 12292
  0.6 14.3 %copy-start.40 = (s32[1,256]{1,0:T(1,128)S(1)}, s32[1,256]{1,0:T(1,128)}, u32[]{:S(2)}) copy-start(s32[1,256]{1,0:T(1,128)} %param.11) | copy-start | bytes 3076
  0.7 14.8 %copy-start.2 = (f32[4,128,256]{2,1,0:T(8,128)S(1)}, f32[4,128,256]{2,1,0:T(8,128)}, u32[]{:S(2)}) copy-start(f32[4,128,256]{2,1,0:T(8,128)} %param.15) | copy-start | bytes 1572868
  2.6 30.9 %collective-permute-start = (f32[3,128,256]{2,1,0:T(8,128)}, f32[3,128,256]{2,1,0:T(8,128)}, u32[]{:S(2)}, u32[]{:S(2)}) collective-permute-start(f32[3,128,256]{2,1,0:T(8,128)} %pad_maximum_fusion.14), channel_id=1, source_target_pairs={{0,4},{4,8},{8,12},{12,16},{16,20},{20,24},{24,28},{28,32},{32,36}... | collective-permute-start | bytes 1179656 | tf_op jit(solution)/shard_map/ppermute | solution.py:17
  19.2 4.9 %copy-start.38 = (f32[1,1,256]{2,1,0:T(1,128)S(1)}, f32[1,1,256]{2,1,0:T(1,128)}, u32[]{:S(2)}) copy-start(f32[1,1,256]{2,1,0:T(1,128)} %get-tuple-element.117) | copy-start | bytes 3076
  23.2 0.8 copy-start.28
  25.4 26.3 %slice-start = ((s8[4718592]{0:T(1024)(128)(4,1)}), s8[524288]{0:T(1024)(128)(4,1)S(1)}, s32[]{:S(2)}) async-start(s8[4718592]{0:T(1024)(128)(4,1)} %bitcast.343), calls=%async_computation | async-start | bytes 1048576
  25.4 8.1 %copy-start.30 = (f32[4,128,256]{2,1,0:T(8,128)S(1)}, f32[4,128,256]{2,1,0:T(8,128)}, u32[]{:S(2)}) copy-start(f32[4,128,256]{2,1,0:T(8,128)} %get-tuple-element.113) | copy-start | bytes 1572868
  25.4 26.3 %slice-start.1 = ((s8[4718592]{0:T(1024)(128)(4,1)}), s8[4194304]{0:T(1024)(128)(4,1)S(1)}, s32[]{:S(2)}) async-start(s8[4718592]{0:T(1024)(128)(4,1)} %bitcast.343), calls=%async_computation.1 | async-start | bytes 8388608
  34.7 22.8 %copy-start.13 = (f32[1,128,256]{2,1,0:T(8,128)}, f32[1,128,256]{2,1,0:T(8,128)S(1)}, u32[]{:S(2)}) copy-start(f32[1,128,256]{2,1,0:T(8,128)S(1)} %get-tuple-element.99) | copy-start | bytes 393220
  34.7 17.1 %copy-start = (f32[4,128,256]{2,1,0:T(8,128)S(1)}, f32[4,128,256]{2,1,0:T(8,128)}, u32[]{:S(2)}) copy-start(f32[4,128,256]{2,1,0:T(8,128)} %param.14) | copy-start | bytes 1572868
  34.7 16.9 %collective-permute-start.1 = (f32[4,128,256]{2,1,0:T(8,128)S(1)}, f32[4,128,256]{2,1,0:T(8,128)S(1)}, u32[]{:S(2)}, u32[]{:S(2)}) collective-permute-start(f32[4,128,256]{2,1,0:T(8,128)S(1)} %pad_maximum_fusion.13), channel_id=1, source_target_pairs={{4,0},{8,4},{12,8},{16,12},{20,16},{24,20},{28,24},{32,28},{36,32}... | collective-permute-start | bytes 1572872 | tf_op jit(solution)/shard_map/ppermute | solution.py:17
  36.5 19.7 %copy-start.6 = (f32[4,127,256]{2,1,0:T(8,128)}, f32[4,127,256]{2,1,0:T(8,128)S(1)}, u32[]{:S(2)}) copy-start(f32[4,127,256]{2,1,0:T(8,128)S(1)} %get-tuple-element.125) | copy-start | bytes 1560580
  36.8 20.7 %copy-start.8 = (f32[4,128,255]{2,1,0:T(8,128)}, f32[4,128,255]{2,1,0:T(8,128)S(1)}, u32[]{:S(2)}) copy-start(f32[4,128,255]{2,1,0:T(8,128)S(1)} %get-tuple-element.122) | copy-start | bytes 1566724
  36.9 16.2 %copy-start.1 = (f32[4,128,256]{2,1,0:T(8,128)S(1)}, f32[4,128,256]{2,1,0:T(8,128)}, u32[]{:S(2)}) copy-start(f32[4,128,256]{2,1,0:T(8,128)} %param.13) | copy-start | bytes 1572868
  51.7 1.7 copy-start.34
  53.4 4.1 %copy-start.23 = (f32[4,128,256]{2,1,0:T(8,128)}, f32[4,128,256]{2,1,0:T(8,128)S(1)}, u32[]{:S(2)}) copy-start(f32[4,128,256]{2,1,0:T(8,128)S(1)} %get-tuple-element.28) | copy-start | bytes 1572868
  53.5 9.9 %collective-permute-start.2 = (f32[3,128,256]{2,1,0:T(8,128)S(1)}, f32[3,128,256]{2,1,0:T(8,128)S(1)}, u32[]{:S(2)}, u32[]{:S(2)}) collective-permute-start(f32[3,128,256]{2,1,0:T(8,128)S(1)} %pad_maximum_fusion.15), channel_id=1, source_target_pairs={{0,4},{4,8},{8,12},{12,16},{16,20},{20,24},{24,28},{28,32},{32,36}... | collective-permute-start | bytes 1179656 | tf_op jit(solution)/shard_map/ppermute | solution.py:17
  57.5 1.0 copy-start.29
  63.5 22.5 %copy-start.14 = (f32[1,128,256]{2,1,0:T(8,128)}, f32[1,128,256]{2,1,0:T(8,128)S(1)}, u32[]{:S(2)}) copy-start(f32[1,128,256]{2,1,0:T(8,128)S(1)} %get-tuple-element.96) | copy-start | bytes 393220
  63.8 13.0 %collective-permute-start.3 = (f32[3,128,256]{2,1,0:T(8,128)S(1)}, f32[3,128,256]{2,1,0:T(8,128)S(1)}, u32[]{:S(2)}, u32[]{:S(2)}) collective-permute-start(f32[3,128,256]{2,1,0:T(8,128)S(1)} %pad_maximum_fusion.16), channel_id=1, source_target_pairs={{4,0},{8,4},{12,8},{16,12},{20,16},{24,20},{28,24},{32,28},{36,32}... | collective-permute-start | bytes 1179656 | tf_op jit(solution)/shard_map/ppermute | solution.py:17
  65.3 19.4 %copy-start.9 = (f32[4,127,256]{2,1,0:T(8,128)}, f32[4,127,256]{2,1,0:T(8,128)S(1)}, u32[]{:S(2)}) copy-start(f32[4,127,256]{2,1,0:T(8,128)S(1)} %fusion.14) | copy-start | bytes 1560580
  65.6 19.1 %copy-start.10 = (f32[4,128,255]{2,1,0:T(8,128)}, f32[4,128,255]{2,1,0:T(8,128)S(1)}, u32[]{:S(2)}) copy-start(f32[4,128,255]{2,1,0:T(8,128)S(1)} %fusion.12) | copy-start | bytes 1566724
  76.9 1.7 copy-start.35
  78.5 7.5 %copy-start.24 = (f32[4,128,256]{2,1,0:T(8,128)}, f32[4,128,256]{2,1,0:T(8,128)S(1)}, u32[]{:S(2)}) copy-start(f32[4,128,256]{2,1,0:T(8,128)S(1)} %get-tuple-element.20) | copy-start | bytes 1572868
  78.6 11.6 %collective-permute-start.4 = (f32[3,128,256]{2,1,0:T(8,128)S(1)}, f32[3,128,256]{2,1,0:T(8,128)S(1)}, u32[]{:S(2)}, u32[]{:S(2)}) collective-permute-start(f32[3,128,256]{2,1,0:T(8,128)S(1)} %pad_maximum_fusion.17), channel_id=1, source_target_pairs={{0,4},{4,8},{8,12},{12,16},{16,20},{20,24},{24,28},{28,32},{32,36}... | collective-permute-start | bytes 1179656 | tf_op jit(solution)/shard_map/ppermute | solution.py:17
  90.3 12.3 %copy-start.12 = (f32[4,127,256]{2,1,0:T(8,128)}, f32[4,127,256]{2,1,0:T(8,128)S(1)}, u32[]{:S(2)}) copy-start(f32[4,127,256]{2,1,0:T(8,128)S(1)} %fusion.8) | copy-start | bytes 1560580
  90.6 11.6 %collective-permute-start.5 = (f32[3,128,256]{2,1,0:T(8,128)S(1)}, f32[3,128,256]{2,1,0:T(8,128)S(1)}, u32[]{:S(2)}, u32[]{:S(2)}) collective-permute-start(f32[3,128,256]{2,1,0:T(8,128)S(1)} %pad_maximum_fusion.18), channel_id=1, source_target_pairs={{4,0},{8,4},{12,8},{16,12},{20,16},{24,20},{28,24},{32,28},{36,32}... | collective-permute-start | bytes 1179656 | tf_op jit(solution)/shard_map/ppermute | solution.py:17
  92.2 10.3 %copy-start.25 = (f32[4,128,255]{2,1,0:T(8,128)}, f32[4,128,255]{2,1,0:T(8,128)S(1)}, u32[]{:S(2)}) copy-start(f32[4,128,255]{2,1,0:T(8,128)S(1)} %fusion.6) | copy-start | bytes 1566724
  102.3 0.7 copy-start.27
  102.6 1.4 copy-start.26
  102.9 9.6 %copy-start.4 = (f32[4,128,256]{2,1,0:T(8,128)}, f32[4,128,256]{2,1,0:T(8,128)S(1)}, u32[]{:S(2)}) copy-start(f32[4,128,256]{2,1,0:T(8,128)S(1)} %get-tuple-element.61) | copy-start | bytes 1572868
  105.4 11.6 %collective-permute-start.6 = (f32[3,128,256]{2,1,0:T(8,128)S(1)}, f32[3,128,256]{2,1,0:T(8,128)S(1)}, u32[]{:S(2)}, u32[]{:S(2)}) collective-permute-start(f32[3,128,256]{2,1,0:T(8,128)S(1)} %pad_maximum_fusion.19), channel_id=1, source_target_pairs={{0,4},{4,8},{8,12},{12,16},{16,20},{20,24},{24,28},{28,32},{32,36}... | collective-permute-start | bytes 1179656 | tf_op jit(solution)/shard_map/ppermute | solution.py:17
  113.0 18.5 %copy-start.3 = (f32[1,1,6,4,128,256]{5,4,3,2,1,0:T(8,128)S(1)}, f32[1,1,6,4,128,256]{5,4,3,2,1,0:T(8,128)}, u32[]{:S(2)}) copy-start(f32[1,1,6,4,128,256]{5,4,3,2,1,0:T(8,128)} %get-tuple-element.36) | copy-start | bytes 9437188
  113.0 18.5 %copy-start.7 = (f32[4,127,256]{2,1,0:T(8,128)S(1)}, f32[4,127,256]{2,1,0:T(8,128)}, u32[]{:S(2)}) copy-start(f32[4,127,256]{2,1,0:T(8,128)} %copy-done.6) | copy-start | bytes 1560580
  117.1 6.1 %copy-start.15 = (f32[1,128,256]{2,1,0:T(8,128)}, f32[1,128,256]{2,1,0:T(8,128)S(1)}, u32[]{:S(2)}) copy-start(f32[1,128,256]{2,1,0:T(8,128)S(1)} %get-tuple-element.82) | copy-start | bytes 393220
  117.1 7.1 %copy-start.17 = (f32[1,128,256]{2,1,0:T(8,128)}, f32[1,128,256]{2,1,0:T(8,128)S(1)}, u32[]{:S(2)}) copy-start(f32[1,128,256]{2,1,0:T(8,128)S(1)} %get-tuple-element.83) | copy-start | bytes 393220
  117.1 13.6 %copy-start.19 = (f32[1,128,256]{2,1,0:T(8,128)}, f32[1,128,256]{2,1,0:T(8,128)S(1)}, u32[]{:S(2)}) copy-start(f32[1,128,256]{2,1,0:T(8,128)S(1)} %get-tuple-element.84) | copy-start | bytes 393220
  119.0 11.6 %collective-permute-start.7 = (f32[3,128,256]{2,1,0:T(8,128)S(1)}, f32[3,128,256]{2,1,0:T(8,128)S(1)}, u32[]{:S(2)}, u32[]{:S(2)}) collective-permute-start(f32[3,128,256]{2,1,0:T(8,128)S(1)} %pad_maximum_fusion.20), channel_id=1, source_target_pairs={{4,0},{8,4},{12,8},{16,12},{20,16},{24,20},{28,24},{32,28},{36,32}... | collective-permute-start | bytes 1179656 | tf_op jit(solution)/shard_map/ppermute | solution.py:17
  141.7 6.3 %copy-start.11 = (f32[4,128,256]{2,1,0:T(8,128)S(1)}, f32[4,128,256]{2,1,0:T(8,128)}, u32[]{:S(2)}) copy-start(f32[4,128,256]{2,1,0:T(8,128)} %get-tuple-element.10) | copy-start | bytes 1572868
  141.7 6.3 %copy-start.20 = (f32[1,128,256]{2,1,0:T(8,128)S(1)}, f32[1,128,256]{2,1,0:T(8,128)}, u32[]{:S(2)}) copy-start(f32[1,128,256]{2,1,0:T(8,128)} %copy-done.19) | copy-start | bytes 393220
  141.7 6.3 %copy-start.36 = (f32[1,128,256]{2,1,0:T(8,128)S(1)}, f32[1,128,256]{2,1,0:T(8,128)}, u32[]{:S(2)}) copy-start(f32[1,128,256]{2,1,0:T(8,128)} %get-tuple-element.81) | copy-start | bytes 393220
  141.7 6.5 %copy-start.5 = (f32[4,128,256]{2,1,0:T(8,128)S(1)}, f32[4,128,256]{2,1,0:T(8,128)}, u32[]{:S(2)}) copy-start(f32[4,128,256]{2,1,0:T(8,128)} %copy-done.4) | copy-start | bytes 1572868
  141.7 6.5 %copy-start.18 = (f32[1,128,256]{2,1,0:T(8,128)S(1)}, f32[1,128,256]{2,1,0:T(8,128)}, u32[]{:S(2)}) copy-start(f32[1,128,256]{2,1,0:T(8,128)} %copy-done.17) | copy-start | bytes 393220
  141.7 6.5 %copy-start.22 = (f32[4,127,256]{2,1,0:T(8,128)S(1)}, f32[4,127,256]{2,1,0:T(8,128)}, u32[]{:S(2)}) copy-start(f32[4,127,256]{2,1,0:T(8,128)} %fusion.2) | copy-start | bytes 1560580
  141.8 3.0 %collective-permute-start.8 = (f32[4,128,256]{2,1,0:T(8,128)}, f32[4,128,256]{2,1,0:T(8,128)S(1)}, u32[]{:S(2)}, u32[]{:S(2)}) collective-permute-start(f32[4,128,256]{2,1,0:T(8,128)} %get-tuple-element.4), channel_id=1, source_target_pairs={{0,1},{1,0},{2,3},{3,2},{4,5},{5,4},{6,7},{7,6},{8,9},{9,8},{10,11... | collective-permute-start | bytes 1572872 | tf_op jit(solution)/shard_map/ppermute | solution.py:139
  146.0 26.3 %copy-start.16 = (f32[1,128,256]{2,1,0:T(8,128)S(1)}, f32[1,128,256]{2,1,0:T(8,128)}, u32[]{:S(2)}) copy-start(f32[1,128,256]{2,1,0:T(8,128)} %copy-done.15) | copy-start | bytes 393220
  146.0 26.3 %copy-start.21 = (f32[4,128,255]{2,1,0:T(8,128)S(1)}, f32[4,128,255]{2,1,0:T(8,128)}, u32[]{:S(2)}) copy-start(f32[4,128,255]{2,1,0:T(8,128)} %fusion) | copy-start | bytes 1566724
  146.0 14.5 %collective-permute-start.9 = (f32[4,128,256]{2,1,0:T(8,128)S(1)}, f32[4,128,256]{2,1,0:T(8,128)S(1)}, u32[]{:S(2)}, u32[]{:S(2)}) collective-permute-start(f32[4,128,256]{2,1,0:T(8,128)S(1)} %select_add_fusion), channel_id=1, source_target_pairs={{0,2},{2,0},{1,3},{3,1},{4,6},{6,4},{5,7},{7,5},{8,10},{10,8},{9,1... | collective-permute-start | bytes 1572872 | tf_op jit(solution)/shard_map/ppermute | solution.py:140
  148.2 34.9 %copy-start.33 = (f32[4,128,256]{2,1,0:T(8,128)S(1)}, f32[4,128,256]{2,1,0:T(8,128)}, u32[]{:S(2)}) copy-start(f32[4,128,256]{2,1,0:T(8,128)} %get-tuple-element.9) | copy-start | bytes 1572868
  148.2 42.6 %copy-start.32 = (f32[4,128,256]{2,1,0:T(8,128)S(1)}, f32[4,128,256]{2,1,0:T(8,128)}, u32[]{:S(2)}) copy-start(f32[4,128,256]{2,1,0:T(8,128)} %get-tuple-element.8) | copy-start | bytes 1572868
  148.4 43.9 %copy-start.31 = (f32[4,128,256]{2,1,0:T(8,128)S(1)}, f32[4,128,256]{2,1,0:T(8,128)}, u32[]{:S(2)}) copy-start(f32[4,128,256]{2,1,0:T(8,128)} %get-tuple-element.7) | copy-start | bytes 1572868
  161.8 10.7 %collective-permute-start.11 = (f32[8,128]{1,0:T(8,128)S(1)}, f32[8,128]{1,0:T(8,128)S(1)}, u32[]{:S(2)}, u32[]{:S(2)}) collective-permute-start(f32[8,128]{1,0:T(8,128)S(1)} %broadcast_in_dim.5), channel_id=1, source_target_pairs={{0,8},{4,12},{8,16},{12,20},{16,24},{20,28},{24,0},{28,4},{32,40},... | collective-permute-start | bytes 12296 | tf_op jit(solution)/shard_map/ppermute | solution.py:127
  166.1 7.8 %collective-permute-start.12 = (f32[8,128]{1,0:T(8,128)S(1)}, f32[8,128]{1,0:T(8,128)S(1)}, u32[]{:S(2)}, u32[]{:S(2)}) collective-permute-start(f32[8,128]{1,0:T(8,128)S(1)} %broadcast_in_dim.5), channel_id=1, source_target_pairs={{0,16},{4,20},{8,24},{12,28},{16,0},{20,4},{24,8},{28,12},{32,48},... | collective-permute-start | bytes 12296 | tf_op jit(solution)/shard_map/ppermute | solution.py:127
  172.2 3.6 %collective-permute-start.13 = (f32[8,128]{1,0:T(8,128)S(1)}, f32[8,128]{1,0:T(8,128)S(1)}, u32[]{:S(2)}, u32[]{:S(2)}) collective-permute-start(f32[8,128]{1,0:T(8,128)S(1)} %broadcast_in_dim.5), channel_id=1, source_target_pairs={{0,24},{4,28},{8,0},{12,4},{16,8},{20,12},{24,16},{28,20},{32,56},... | collective-permute-start | bytes 12296 | tf_op jit(solution)/shard_map/ppermute | solution.py:127
  176.5 6.8 %collective-permute-start.14 = (f32[8,128]{1,0:T(8,128)S(1)}, f32[8,128]{1,0:T(8,128)S(1)}, u32[]{:S(2)}, u32[]{:S(2)}) collective-permute-start(f32[8,128]{1,0:T(8,128)S(1)} %maximum_maximum_fusion.1), channel_id=1, source_target_pairs={{0,32},{4,36},{8,40},{12,44},{16,48},{20,52},{24,56},{28,60},{32,6... | collective-permute-start | bytes 12296 | tf_op jit(solution)/shard_map/ppermute | solution.py:127
  178.9 5.1 %collective-permute-start.15 = (f32[8,128]{1,0:T(8,128)S(1)}, f32[8,128]{1,0:T(8,128)S(1)}, u32[]{:S(2)}, u32[]{:S(2)}) collective-permute-start(f32[8,128]{1,0:T(8,128)S(1)} %maximum_maximum_fusion.1), channel_id=1, source_target_pairs={{0,64},{4,68},{8,72},{12,76},{16,80},{20,84},{24,88},{28,92},{32,9... | collective-permute-start | bytes 12296 | tf_op jit(solution)/shard_map/ppermute | solution.py:127
  182.1 3.6 %collective-permute-start.16 = (f32[8,128]{1,0:T(8,128)S(1)}, f32[8,128]{1,0:T(8,128)S(1)}, u32[]{:S(2)}, u32[]{:S(2)}) collective-permute-start(f32[8,128]{1,0:T(8,128)S(1)} %maximum_maximum_fusion.1), channel_id=1, source_target_pairs={{0,96},{4,100},{8,104},{12,108},{16,112},{20,116},{24,120},{28,124... | collective-permute-start | bytes 12296 | tf_op jit(solution)/shard_map/ppermute | solution.py:127
  183.2 13.1 %collective-permute-start.10 = (f32[4,128,256]{2,1,0:T(8,128)S(1)}, f32[4,128,256]{2,1,0:T(8,128)S(1)}, u32[]{:S(2)}, u32[]{:S(2)}) collective-permute-start(f32[4,128,256]{2,1,0:T(8,128)S(1)} %get-tuple-element.3), channel_id=1, source_target_pairs={{0,1},{1,0},{2,3},{3,2},{4,5},{5,4},{6,7},{7,6},{8,9},{9,8},{10,11... | collective-permute-start | bytes 1572872 | tf_op jit(solution)/shard_map/ppermute | solution.py:141
  185.7 6.6 %collective-permute-start.17 = (f32[8,128]{1,0:T(8,128)S(1)}, f32[8,128]{1,0:T(8,128)S(1)}, u32[]{:S(2)}, u32[]{:S(2)}) collective-permute-start(f32[8,128]{1,0:T(8,128)S(1)} %maximum_maximum_fusion), channel_id=1, source_target_pairs={{0,4},{4,0},{8,12},{12,8},{16,20},{20,16},{24,28},{28,24},{32,36},... | collective-permute-start | bytes 12296 | tf_op jit(solution)/shard_map/ppermute | solution.py:127
  192.4 1.2 collective-permute-start.18
  192.5 5.1 %copy-start.37 = (f32[9,4,128,256]{3,2,1,0:T(8,128)}, f32[9,4,128,256]{3,2,1,0:T(8,128)S(1)}, u32[]{:S(2)}) copy-start(f32[9,4,128,256]{3,2,1,0:T(8,128)S(1)} %bitcast_dynamic-update-slice_fusion) | copy-start | bytes 14155780

commit v3 on v2

--- a/solution.py
+++ b/solution.py
@@ -82,11 +82,12 @@
             + amount.reshape(shape),
         ]
         last = [stress[0][-1], stress[3][-1], stress[4][-1]]
-        left = shifted(jnp.stack(last), "space", 1)
         firsts = [p[0] for p in part]
         if step == 0:
             firsts = firsts + [factor[0]]
-        right = shifted(jnp.stack(firsts), "space", -1)
+        ahead, behind = lax.optimization_barrier((jnp.stack(last), jnp.stack(firsts)))
+        right = shifted(behind, "space", -1)
+        left = shifted(ahead, "space", 1)
         if step == 0:
             factor_right = right[3]
         velocity = [
@@ -113,6 +114,8 @@
         grad_shear = grad_shear + solid * (
             2.0 * (exx * fwd[0] + eyy * fwd[1] + ezz * fwd[2]) + gxy * fwd[3] + gxz * fwd[4] + gyz * fwd[5]
         )
+        if step < STEPS - 1:
+            grad_lam, grad_shear = lax.optimization_barrier((grad_lam, grad_shear))
     final_state = jnp.stack(velocity + stress)[None]
     return (final_state, updated_model(grad_lam, grad_shear, lame_lambda, lame_mu))
 

time: 199 us -> 188 us (0.945)
  other arithmetic: 53.6 us -> 39.6 us
  local copies, waits for them, and re-layouts: 12.2 us -> 16.4 us
  waiting for transfers between devices: 73.9 us -> 70.2 us
  starting transfers between devices: 51.6 us -> 54.6 us
    select_n x1, other arithmetic: 10.2 us -> 1.06 us  [updated_model(): give = jnp.where(even, grad_shear, grad_lam)]
    ppermute x8, waiting for transfers between devices: 53.6 us -> 46.4 us  [shifted(): return lax.ppermute(block, axis, route)]
    concatenate x22, other arithmetic: 7.83 us -> 2.86 us  [shards(): jnp.concatenate([(part[k][0] - factor[0] * left[k])[None], part[k][1:]],...]
    add x2 -> x4, other arithmetic: 2.44 us -> 6.45 us  [shards(): velocity[1]]
    ppermute x8, starting transfers between devices: 27.3 us -> 31.3 us  [shifted(): return lax.ppermute(block, axis, route)]
    sub x4, other arithmetic: 0.98 us -> 4.22 us  [shards(): beyond = [right[k] - factor_right * last[k] for k in range(3)]]
    slice x12, local copies, waits for them, and re-layouts: 0.33 us -> 3.52 us  [shards(): part[k][1:]]
    unnamed x9 -> x10, other arithmetic: 3.76 us -> 0.91 us
  transfers between devices with their start and end apart: 19 -> 19, of which waited for: 14 -> 11; matrix products, arithmetic and copies ran while one was open for 20% -> 10% of each run, Pallas kernels for 0% -> 0%
where the time goes in v3:
time: 188 us; the launch traced here: 187 us
  waiting for transfers between devices  70.2 us (37%)
  starting transfers between devices  54.6 us (29%)
  other arithmetic  39.6 us (21%)
  local copies, waits for them, and re-layouts  16.4 us (9%)
  between operations  3.76 us (2%)
  matrix products  1.96 us (1%)
    ppermute x8, waiting for transfers between devices, shifted(): return lax.ppermute(block, axis, route)  46.4 us
    ppermute x8, starting transfers between devices, shifted(): return lax.ppermute(block, axis, route)  31.3 us
    ppermute x7, starting transfers between devices, space_peak(): arrived.append(lax.ppermute(value, 'space', route))  21.1 us
    ppermute x1, waiting for transfers between devices, updated_model(): total = half + lax.ppermute(half, 'shot', across)  11.8 us
    ppermute x7, waiting for transfers between devices, space_peak(): arrived.append(lax.ppermute(value, 'space', route))  9.2 us
    add x4, other arithmetic, shards(): velocity[1]  6.45 us
    convert_element_type x1, other arithmetic, shards(): fwd = strains[step].astype(jnp.float32)  5.47 us
    sub x4, other arithmetic, shards(): beyond = [right[k] - factor_right * last[k] for k in range(3)]  4.22 us
  transfers between devices with their start and end apart: 19, of which 11 were waited for; matrix products, arithmetic and copies ran while one was open for 10% of the time, Pallas kernels for 0%

profile of v3, /device:TPU:0, one launch (start us, length us, event | category | flops | bytes accessed | tf_op | source)
XLA Modules:
  0.0 186.5 jit_solution(913629137254279917)
XLA Ops:
  0.7 2.9 %slice_bitcast_fusion.26 = (f32[4,128,256]{2,1,0:T(8,128)}, f32[4,128,256]{2,1,0:T(8,128)S(1)}, f32[4,128,256]{2,1,0:T(8,128)S(1)}, f32[4,128,256]{2,1,0:T(8,128)}, f32[4,128,256]{2,1,0:T(8,128)}) fusion(f32[1,9,4,128,256]{4,3,2,1,0:T(8,128)} %param.8), kind=kLoop, calls=%fused_computation.240 | loop fusion | bytes 5242880 | tf_op jit(solution)/shard_map/squeeze | solution.py:70
  3.6 2.3 %slice_bitcast_fusion.30 = (f32[3,128,256]{2,1,0:T(8,128)}, f32[3,128,256]{2,1,0:T(8,128)}, f32[3,128,256]{2,1,0:T(8,128)}) fusion(f32[1,9,4,128,256]{4,3,2,1,0:T(8,128)} %param.8), kind=kLoop, calls=%fused_computation.253 | loop fusion | bytes 2359296 | tf_op jit(solution)/shard_map/slice | solution.py:45
  5.9 1.1 slice_bitcast_fusion.34
  7.0 0.6 fusion.117
  7.6 0.5 fusion.71
  8.1 3.4 %bitcast_add_fusion.1 = (f32[4,128,256]{2,1,0:T(8,128)S(1)}, f32[4,128,256]{2,1,0:T(8,128)S(1)}, f32[4,128,256]{2,1,0:T(8,128)S(1)}) fusion(f32[4,128,255]{2,1,0:T(8,128)S(1)} %bitcast.338, f32[4,127,256]{2,1,0:T(8,128)} %bitcast.342, f32[3,128,256]{2,1,0:T(8,128)} %get-tuple-element.72, f32[1,9,4,128,256]{4,3,2,1,0:T(8,128)} %param.8, ...), kind=kLoop, calls=%fused_computation.176 | loop fusion | flops 2097152 | bytes 9162752 | tf_op jit(solution)/shard_map/add | solution.py:80
  11.6 2.5 %fusion.67 = f32[4,128,256]{2,1,0:T(8,128)S(1)} fusion(f32[4,128,255]{2,1,0:T(8,128)S(1)} %bitcast.340, f32[4,127,256]{2,1,0:T(8,128)S(1)} %bitcast.341, f32[3,128,256]{2,1,0:T(8,128)S(1)} %copy-done.20, f32[1,9,4,128,256]{4,3,2,1,0:T(8,128)} %param.8, f32[4,128,256]{2,1,0:T(8,128)S(1)} %copy-done.1), kind=kLoop, calls=%fused_computation.182 | loop fusion | flops 1048576 | bytes 4581376 | tf_op jit(solution)/shard_map/add | solution.py:79
  14.1 0.8 pad_maximum_fusion.14
  14.9 0.8 pad_maximum_fusion.13
  15.8 6.8 %collective-permute-start = (f32[3,128,256]{2,1,0:T(8,128)}, f32[3,128,256]{2,1,0:T(8,128)}, u32[]{:S(2)}, u32[]{:S(2)}) collective-permute-start(f32[3,128,256]{2,1,0:T(8,128)} %pad_maximum_fusion.14), channel_id=1, source_target_pairs={{0,4},{4,8},{8,12},{12,16},{16,20},{20,24},{24,28},{28,32},{32,36}... | collective-permute-start | bytes 1179656 | tf_op jit(solution)/shard_map/ppermute | solution.py:17
  22.6 1.3 collective-permute-start.1
  23.9 5.5 %slice_convert_fusion = (f32[1,1,6,4,128,256]{5,4,3,2,1,0:T(8,128)}, f32[1,1,6,4,128,256]{5,4,3,2,1,0:T(8,128)}, f32[1,1,6,4,128,256]{5,4,3,2,1,0:T(8,128)}, f32[1,1,6,4,128,256]{5,4,3,2,1,0:T(8,128)}) fusion(bf16[1,4,6,4,128,256]{5,4,3,2,1,0:T(8,128)(2,1)S(1)} %bitcast.337), kind=kLoop, calls=%fused_computation | loop fusion | flops 3145728 | bytes 18874368 | tf_op jit(solution)/shard_map/convert_element_type | solution.py:97
  29.5 0.6 dynamic_slice.4
  31.2 10.5 %collective-permute-done = f32[3,128,256]{2,1,0:T(8,128)} collective-permute-done((f32[3,128,256]{2,1,0:T(8,128)}, f32[3,128,256]{2,1,0:T(8,128)}, u32[]{:S(2)}, u32[]{:S(2)}) %collective-permute-start) | collective-permute-done | bytes 393248 | tf_op jit(solution)/shard_map/ppermute | solution.py:17
  41.7 1.2 fusion.89
  43.6 1.3 slice_subtract_fusion.9
  45.3 0.8 fusion.50
  46.1 1.0 slice-done
  47.7 0.7 multiply_add_fusion.22
  49.0 0.7 multiply_add_fusion.20
  49.8 5.9 %collective-permute-start.2 = (f32[3,128,256]{2,1,0:T(8,128)S(1)}, f32[3,128,256]{2,1,0:T(8,128)S(1)}, u32[]{:S(2)}, u32[]{:S(2)}) collective-permute-start(f32[3,128,256]{2,1,0:T(8,128)S(1)} %pad_maximum_fusion.15), channel_id=1, source_target_pairs={{0,4},{4,8},{8,12},{12,16},{16,20},{20,24},{24,28},{28,32},{32,36}... | collective-permute-start | bytes 1179656 | tf_op jit(solution)/shard_map/ppermute | solution.py:17
  56.4 1.7 collective-permute-start.3
  58.1 13.5 %collective-permute-done.2 = f32[3,128,256]{2,1,0:T(8,128)S(1)} collective-permute-done((f32[3,128,256]{2,1,0:T(8,128)S(1)}, f32[3,128,256]{2,1,0:T(8,128)S(1)}, u32[]{:S(2)}, u32[]{:S(2)}) %collective-permute-start.2) | collective-permute-done | bytes 393248 | tf_op jit(solution)/shard_map/ppermute | solution.py:17
  72.5 1.0 slice_subtract_fusion.6
  73.8 0.8 fusion.43
  74.6 0.6 multiply_add_fusion.14
  76.1 0.8 multiply_add_fusion.12
  76.9 5.9 %collective-permute-start.4 = (f32[3,128,256]{2,1,0:T(8,128)S(1)}, f32[3,128,256]{2,1,0:T(8,128)S(1)}, u32[]{:S(2)}, u32[]{:S(2)}) collective-permute-start(f32[3,128,256]{2,1,0:T(8,128)S(1)} %pad_maximum_fusion.17), channel_id=1, source_target_pairs={{0,4},{4,8},{8,12},{12,16},{16,20},{20,24},{24,28},{28,32},{32,36}... | collective-permute-start | bytes 1179656 | tf_op jit(solution)/shard_map/ppermute | solution.py:17
  83.5 1.6 collective-permute-start.5
  85.0 12.9 %collective-permute-done.4 = f32[3,128,256]{2,1,0:T(8,128)S(1)} collective-permute-done((f32[3,128,256]{2,1,0:T(8,128)S(1)}, f32[3,128,256]{2,1,0:T(8,128)S(1)}, u32[]{:S(2)}, u32[]{:S(2)}) %collective-permute-start.4) | collective-permute-done | bytes 393248 | tf_op jit(solution)/shard_map/ppermute | solution.py:17
  98.7 1.0 slice_subtract_fusion.3
  99.7 1.1 multiply_add_fusion.1
  100.9 1.6 fusion.35
  102.5 0.7 multiply_add_fusion.6
  104.3 1.5 multiply_add_fusion.4
  105.8 1.0 slice.881
  106.9 6.7 %collective-permute-start.6 = (f32[3,128,256]{2,1,0:T(8,128)S(1)}, f32[3,128,256]{2,1,0:T(8,128)}, u32[]{:S(2)}, u32[]{:S(2)}) collective-permute-start(f32[3,128,256]{2,1,0:T(8,128)S(1)} %pad_maximum_fusion.19), channel_id=1, source_target_pairs={{0,4},{4,8},{8,12},{12,16},{16,20},{20,24},{24,28},{28,32},{32,36}... | collective-permute-start | bytes 1179656 | tf_op jit(solution)/shard_map/ppermute | solution.py:17
  113.6 1.0 slice.887
  114.6 1.1 slice.889
  115.7 1.2 slice.891
  116.9 1.4 collective-permute-start.7
  118.4 1.3 fusion.80
  120.4 9.5 %collective-permute-done.7 = f32[3,128,256]{2,1,0:T(8,128)S(1)} collective-permute-done((f32[3,128,256]{2,1,0:T(8,128)S(1)}, f32[3,128,256]{2,1,0:T(8,128)S(1)}, u32[]{:S(2)}, u32[]{:S(2)}) %collective-permute-start.7) | collective-permute-done | bytes 393248 | tf_op jit(solution)/shard_map/ppermute | solution.py:17
  130.0 1.0 slice_subtract_fusion.1
  131.0 1.1 broadcast_select_fusion
  132.3 1.8 collective-permute-done.8
  134.1 2.0 %collective-permute-start.9 = (f32[4,128,256]{2,1,0:T(8,128)S(1)}, f32[4,128,256]{2,1,0:T(8,128)S(1)}, u32[]{:S(2)}, u32[]{:S(2)}) collective-permute-start(f32[4,128,256]{2,1,0:T(8,128)S(1)} %select_add_fusion), channel_id=1, source_target_pairs={{0,2},{2,0},{1,3},{3,1},{4,6},{6,4},{5,7},{7,5},{8,10},{10,8},{9,1... | collective-permute-start | bytes 1572872 | tf_op jit(solution)/shard_map/ppermute | solution.py:143
  136.5 11.8 %collective-permute-done.9 = f32[4,128,256]{2,1,0:T(8,128)S(1)} collective-permute-done((f32[4,128,256]{2,1,0:T(8,128)S(1)}, f32[4,128,256]{2,1,0:T(8,128)S(1)}, u32[]{:S(2)}, u32[]{:S(2)}) %collective-permute-start.9) | collective-permute-done | bytes 524320 | tf_op jit(solution)/shard_map/ppermute | solution.py:143
  148.4 0.7 abs_reduce_fusion
  149.0 0.6 broadcast_in_dim.5
  149.7 8.6 %collective-permute-start.13 = (f32[8,128]{1,0:T(8,128)S(1)}, f32[8,128]{1,0:T(8,128)S(1)}, u32[]{:S(2)}, u32[]{:S(2)}) collective-permute-start(f32[8,128]{1,0:T(8,128)S(1)} %broadcast_in_dim.5), channel_id=1, source_target_pairs={{0,24},{4,28},{8,0},{12,4},{16,8},{20,12},{24,16},{28,20},{32,56},... | collective-permute-start | bytes 12296 | tf_op jit(solution)/shard_map/ppermute | solution.py:130
  158.3 1.2 collective-permute-start.11
  159.6 3.7 %collective-permute-done.12 = f32[8,128]{1,0:T(8,128)S(1)} collective-permute-done((f32[8,128]{1,0:T(8,128)S(1)}, f32[8,128]{1,0:T(8,128)S(1)}, u32[]{:S(2)}, u32[]{:S(2)}) %collective-permute-start.12) | collective-permute-done | bytes 4128 | tf_op jit(solution)/shard_map/ppermute | solution.py:130
  163.4 0.7 maximum_maximum_fusion.1
  164.0 6.6 %collective-permute-start.16 = (f32[8,128]{1,0:T(8,128)S(1)}, f32[8,128]{1,0:T(8,128)S(1)}, u32[]{:S(2)}, u32[]{:S(2)}) collective-permute-start(f32[8,128]{1,0:T(8,128)S(1)} %maximum_maximum_fusion.1), channel_id=1, source_target_pairs={{0,96},{4,100},{8,104},{12,108},{16,112},{20,116},{24,120},{28,124... | collective-permute-start | bytes 12296 | tf_op jit(solution)/shard_map/ppermute | solution.py:130
  170.6 0.6 collective-permute-start.15
  171.3 0.9 collective-permute-start.14
  172.4 3.4 %collective-permute-done.15 = f32[8,128]{1,0:T(8,128)S(1)} collective-permute-done((f32[8,128]{1,0:T(8,128)S(1)}, f32[8,128]{1,0:T(8,128)S(1)}, u32[]{:S(2)}, u32[]{:S(2)}) %collective-permute-start.15) | collective-permute-done | bytes 4128 | tf_op jit(solution)/shard_map/ppermute | solution.py:130
  176.1 3.3 %collective-permute-start.17 = (f32[8,128]{1,0:T(8,128)S(1)}, f32[8,128]{1,0:T(8,128)S(1)}, u32[]{:S(2)}, u32[]{:S(2)}) collective-permute-start(f32[8,128]{1,0:T(8,128)S(1)} %maximum_maximum_fusion), channel_id=1, source_target_pairs={{0,4},{4,0},{8,12},{12,8},{16,20},{20,16},{24,28},{28,24},{32,36},... | collective-permute-start | bytes 12296 | tf_op jit(solution)/shard_map/ppermute | solution.py:130
  179.4 1.8 collective-permute-done.17
  181.3 1.0 collective-permute-done.18
  182.4 1.0 slice.765
  183.4 0.6 slice.766
  185.5 1.0 pad_maximum_fusion
  (169 shorter events, 10.6 us)
Async XLA Ops:
  0.6 6.3 %copy-start.23 = (f32[1,4,256]{2,1,0:T(4,128)S(1)}, f32[1,4,256]{2,1,0:T(4,128)}, u32[]{:S(2)}) copy-start(f32[1,4,256]{2,1,0:T(4,128)} %param.10) | copy-start | bytes 12292
  0.6 6.9 %copy-start.24 = (s32[1,256]{1,0:T(1,128)S(1)}, s32[1,256]{1,0:T(1,128)}, u32[]{:S(2)}) copy-start(s32[1,256]{1,0:T(1,128)} %param.11) | copy-start | bytes 3076
  0.7 7.4 %copy-start.1 = (f32[4,128,256]{2,1,0:T(8,128)S(1)}, f32[4,128,256]{2,1,0:T(8,128)}, u32[]{:S(2)}) copy-start(f32[4,128,256]{2,1,0:T(8,128)} %param.15) | copy-start | bytes 1572868
  8.1 15.8 %slice-start.2 = ((s8[6291456]{0:T(1024)(128)(4,1)}), s8[4194304]{0:T(1024)(128)(4,1)S(1)}, s32[]{:S(2)}) async-start(s8[6291456]{0:T(1024)(128)(4,1)} %bitcast.336), calls=%async_computation.2 | async-start | bytes 8388608
  8.1 3.5 %copy-start.19 = (f32[4,128,256]{2,1,0:T(8,128)S(1)}, f32[4,128,256]{2,1,0:T(8,128)}, u32[]{:S(2)}) copy-start(f32[4,128,256]{2,1,0:T(8,128)} %get-tuple-element.78) | copy-start | bytes 1572868
  8.1 3.5 %copy-start.20 = (f32[3,128,256]{2,1,0:T(8,128)S(1)}, f32[3,128,256]{2,1,0:T(8,128)}, u32[]{:S(2)}) copy-start(f32[3,128,256]{2,1,0:T(8,128)} %get-tuple-element.73) | copy-start | bytes 1179652
  8.1 15.8 %slice-start.3 = ((s8[6291456]{0:T(1024)(128)(4,1)}), s8[2097152]{0:T(1024)(128)(4,1)S(1)}, s32[]{:S(2)}) async-start(s8[6291456]{0:T(1024)(128)(4,1)} %bitcast.336), calls=%async_computation.3 | async-start | bytes 4194304
  11.5 17.8 %copy-start.16 = (f32[4,128,256]{2,1,0:T(8,128)}, f32[4,128,256]{2,1,0:T(8,128)S(1)}, u32[]{:S(2)}) copy-start(f32[4,128,256]{2,1,0:T(8,128)S(1)} %get-tuple-element.71) | copy-start | bytes 1572868
  11.5 86.4 %copy-start.13 = (f32[4,128,256]{2,1,0:T(8,128)}, f32[4,128,256]{2,1,0:T(8,128)S(1)}, u32[]{:S(2)}) copy-start(f32[4,128,256]{2,1,0:T(8,128)S(1)} %get-tuple-element.124) | copy-start | bytes 1572868
  15.8 13.7 %copy-start.25 = (s32[32]{0:T(128)S(1)}, s32[32]{0:T(128)}, u32[]{:S(2)}) copy-start(s32[32]{0:T(128)} %param.12) | copy-start | bytes 388
  15.8 15.0 %copy-start.22 = (f32[1,1,256]{2,1,0:T(1,128)S(1)}, f32[1,1,256]{2,1,0:T(1,128)}, u32[]{:S(2)}) copy-start(f32[1,1,256]{2,1,0:T(1,128)} %get-tuple-element.128) | copy-start | bytes 3076
  15.8 25.9 %collective-permute-start = (f32[3,128,256]{2,1,0:T(8,128)}, f32[3,128,256]{2,1,0:T(8,128)}, u32[]{:S(2)}, u32[]{:S(2)}) collective-permute-start(f32[3,128,256]{2,1,0:T(8,128)} %pad_maximum_fusion.14), channel_id=1, source_target_pairs={{0,4},{4,8},{8,12},{12,16},{16,20},{20,24},{24,28},{28,32},{32,36}... | collective-permute-start | bytes 1179656 | tf_op jit(solution)/shard_map/ppermute | solution.py:17
  22.6 21.0 %collective-permute-start.1 = (f32[4,128,256]{2,1,0:T(8,128)}, f32[4,128,256]{2,1,0:T(8,128)}, u32[]{:S(2)}, u32[]{:S(2)}) collective-permute-start(f32[4,128,256]{2,1,0:T(8,128)} %pad_maximum_fusion.13), channel_id=1, source_target_pairs={{4,0},{8,4},{12,8},{16,12},{20,16},{24,20},{28,24},{32,28},{36,32}... | collective-permute-start | bytes 1572872 | tf_op jit(solution)/shard_map/ppermute | solution.py:17
  30.7 14.2 %copy-start.5 = (f32[1,1,6,4,128,256]{5,4,3,2,1,0:T(8,128)S(1)}, f32[1,1,6,4,128,256]{5,4,3,2,1,0:T(8,128)}, u32[]{:S(2)}) copy-start(f32[1,1,6,4,128,256]{5,4,3,2,1,0:T(8,128)} %get-tuple-element.59) | copy-start | bytes 9437188
  44.9 2.2 %slice-start = ((s8[4718592]{0:T(1024)(128)(4,1)}), s8[4194304]{0:T(1024)(128)(4,1)S(1)}, s32[]{:S(2)}) async-start(s8[4718592]{0:T(1024)(128)(4,1)} %bitcast.316), calls=%async_computation | async-start | bytes 8388608
  45.3 2.0 %copy-start = (f32[4,128,256]{2,1,0:T(8,128)S(1)}, f32[4,128,256]{2,1,0:T(8,128)}, u32[]{:S(2)}) copy-start(f32[4,128,256]{2,1,0:T(8,128)} %param.14) | copy-start | bytes 1572868
  45.3 2.1 %slice-start.1 = ((s8[4718592]{0:T(1024)(128)(4,1)}), s8[524288]{0:T(1024)(128)(4,1)S(1)}, s32[]{:S(2)}) async-start(s8[4718592]{0:T(1024)(128)(4,1)} %bitcast.316), calls=%async_computation.1 | async-start | bytes 1048576
  46.1 1.6 copy-start.2
  49.8 21.8 %collective-permute-start.2 = (f32[3,128,256]{2,1,0:T(8,128)S(1)}, f32[3,128,256]{2,1,0:T(8,128)S(1)}, u32[]{:S(2)}, u32[]{:S(2)}) collective-permute-start(f32[3,128,256]{2,1,0:T(8,128)S(1)} %pad_maximum_fusion.15), channel_id=1, source_target_pairs={{0,4},{4,8},{8,12},{12,16},{16,20},{20,24},{24,28},{28,32},{32,36}... | collective-permute-start | bytes 1179656 | tf_op jit(solution)/shard_map/ppermute | solution.py:17
  56.3 17.1 %copy-start.4 = (f32[1,1,6,4,128,256]{5,4,3,2,1,0:T(8,128)S(1)}, f32[1,1,6,4,128,256]{5,4,3,2,1,0:T(8,128)}, u32[]{:S(2)}) copy-start(f32[1,1,6,4,128,256]{5,4,3,2,1,0:T(8,128)} %get-tuple-element.58) | copy-start | bytes 9437188
  56.4 16.1 %collective-permute-start.3 = (f32[3,128,256]{2,1,0:T(8,128)S(1)}, f32[3,128,256]{2,1,0:T(8,128)S(1)}, u32[]{:S(2)}, u32[]{:S(2)}) collective-permute-start(f32[3,128,256]{2,1,0:T(8,128)S(1)} %pad_maximum_fusion.16), channel_id=1, source_target_pairs={{4,0},{8,4},{12,8},{16,12},{20,16},{24,20},{28,24},{32,28},{36,32}... | collective-permute-start | bytes 1179656 | tf_op jit(solution)/shard_map/ppermute | solution.py:17
  76.9 21.0 %collective-permute-start.4 = (f32[3,128,256]{2,1,0:T(8,128)S(1)}, f32[3,128,256]{2,1,0:T(8,128)S(1)}, u32[]{:S(2)}, u32[]{:S(2)}) collective-permute-start(f32[3,128,256]{2,1,0:T(8,128)S(1)} %pad_maximum_fusion.17), channel_id=1, source_target_pairs={{0,4},{4,8},{8,12},{12,16},{16,20},{20,24},{24,28},{28,32},{32,36}... | collective-permute-start | bytes 1179656 | tf_op jit(solution)/shard_map/ppermute | solution.py:17
  83.4 16.3 %copy-start.3 = (f32[1,1,6,4,128,256]{5,4,3,2,1,0:T(8,128)S(1)}, f32[1,1,6,4,128,256]{5,4,3,2,1,0:T(8,128)}, u32[]{:S(2)}) copy-start(f32[1,1,6,4,128,256]{5,4,3,2,1,0:T(8,128)} %get-tuple-element.60) | copy-start | bytes 9437188
  83.5 15.3 %collective-permute-start.5 = (f32[3,128,256]{2,1,0:T(8,128)S(1)}, f32[3,128,256]{2,1,0:T(8,128)S(1)}, u32[]{:S(2)}, u32[]{:S(2)}) collective-permute-start(f32[3,128,256]{2,1,0:T(8,128)S(1)} %pad_maximum_fusion.18), channel_id=1, source_target_pairs={{4,0},{8,4},{12,8},{16,12},{20,16},{24,20},{28,24},{32,28},{36,32}... | collective-permute-start | bytes 1179656 | tf_op jit(solution)/shard_map/ppermute | solution.py:17
  103.1 0.9 copy-start.9
  103.1 1.0 copy-start.7
  103.1 1.1 copy-start.11
  104.0 1.8 copy-start.14
  105.8 1.0 copy-start.15
  106.9 11.4 %collective-permute-start.6 = (f32[3,128,256]{2,1,0:T(8,128)S(1)}, f32[3,128,256]{2,1,0:T(8,128)}, u32[]{:S(2)}, u32[]{:S(2)}) collective-permute-start(f32[3,128,256]{2,1,0:T(8,128)S(1)} %pad_maximum_fusion.19), channel_id=1, source_target_pairs={{0,4},{4,8},{8,12},{12,16},{16,20},{20,24},{24,28},{28,32},{32,36}... | collective-permute-start | bytes 1179656 | tf_op jit(solution)/shard_map/ppermute | solution.py:17
  114.6 15.3 %copy-start.8 = (f32[4,128,256]{2,1,0:T(8,128)S(1)}, f32[4,128,256]{2,1,0:T(8,128)}, u32[]{:S(2)}) copy-start(f32[4,128,256]{2,1,0:T(8,128)} %copy-done.7) | copy-start | bytes 1572868
  115.7 15.2 %copy-start.6 = (f32[1,1,6,4,128,256]{5,4,3,2,1,0:T(8,128)S(1)}, f32[1,1,6,4,128,256]{5,4,3,2,1,0:T(8,128)}, u32[]{:S(2)}) copy-start(f32[1,1,6,4,128,256]{5,4,3,2,1,0:T(8,128)} %get-tuple-element.57) | copy-start | bytes 9437188
  115.7 15.2 %copy-start.17 = (f32[4,128,256]{2,1,0:T(8,128)S(1)}, f32[4,128,256]{2,1,0:T(8,128)}, u32[]{:S(2)}) copy-start(f32[4,128,256]{2,1,0:T(8,128)} %get-tuple-element.28) | copy-start | bytes 1572868
  115.7 15.2 %copy-start.18 = (f32[4,128,256]{2,1,0:T(8,128)S(1)}, f32[4,128,256]{2,1,0:T(8,128)}, u32[]{:S(2)}) copy-start(f32[4,128,256]{2,1,0:T(8,128)} %get-tuple-element.29) | copy-start | bytes 1572868
  116.9 13.0 %collective-permute-start.7 = (f32[3,128,256]{2,1,0:T(8,128)S(1)}, f32[3,128,256]{2,1,0:T(8,128)S(1)}, u32[]{:S(2)}, u32[]{:S(2)}) collective-permute-start(f32[3,128,256]{2,1,0:T(8,128)S(1)} %pad_maximum_fusion.20), channel_id=1, source_target_pairs={{4,0},{8,4},{12,8},{16,12},{20,16},{24,20},{28,24},{32,28},{36,32}... | collective-permute-start | bytes 1179656 | tf_op jit(solution)/shard_map/ppermute | solution.py:17
  132.0 4.3 %copy-start.12 = (f32[4,128,256]{2,1,0:T(8,128)S(1)}, f32[4,128,256]{2,1,0:T(8,128)}, u32[]{:S(2)}) copy-start(f32[4,128,256]{2,1,0:T(8,128)} %copy-done.11) | copy-start | bytes 1572868
  132.0 2.0 %collective-permute-start.8 = (f32[4,128,256]{2,1,0:T(8,128)S(1)}, f32[4,128,256]{2,1,0:T(8,128)S(1)}, u32[]{:S(2)}, u32[]{:S(2)}) collective-permute-start(f32[4,128,256]{2,1,0:T(8,128)S(1)} %get-tuple-element.32), channel_id=1, source_target_pairs={{0,1},{1,0},{2,3},{3,2},{4,5},{5,4},{6,7},{7,6},{8,9},{9,8},{10,11... | collective-permute-start | bytes 1572872 | tf_op jit(solution)/shard_map/ppermute | solution.py:142
  134.1 25.3 %copy-start.10 = (f32[4,128,256]{2,1,0:T(8,128)S(1)}, f32[4,128,256]{2,1,0:T(8,128)}, u32[]{:S(2)}) copy-start(f32[4,128,256]{2,1,0:T(8,128)} %copy-done.9) | copy-start | bytes 1572868
  134.1 14.2 %collective-permute-start.9 = (f32[4,128,256]{2,1,0:T(8,128)S(1)}, f32[4,128,256]{2,1,0:T(8,128)S(1)}, u32[]{:S(2)}, u32[]{:S(2)}) collective-permute-start(f32[4,128,256]{2,1,0:T(8,128)S(1)} %select_add_fusion), channel_id=1, source_target_pairs={{0,2},{2,0},{1,3},{3,1},{4,6},{6,4},{5,7},{7,5},{8,10},{10,8},{9,1... | collective-permute-start | bytes 1572872 | tf_op jit(solution)/shard_map/ppermute | solution.py:143
  149.7 10.0 %collective-permute-start.13 = (f32[8,128]{1,0:T(8,128)S(1)}, f32[8,128]{1,0:T(8,128)S(1)}, u32[]{:S(2)}, u32[]{:S(2)}) collective-permute-start(f32[8,128]{1,0:T(8,128)S(1)} %broadcast_in_dim.5), channel_id=1, source_target_pairs={{0,24},{4,28},{8,0},{12,4},{16,8},{20,12},{24,16},{28,20},{32,56},... | collective-permute-start | bytes 12296 | tf_op jit(solution)/shard_map/ppermute | solution.py:130
  158.3 5.1 %collective-permute-start.12 = (f32[8,128]{1,0:T(8,128)S(1)}, f32[8,128]{1,0:T(8,128)S(1)}, u32[]{:S(2)}, u32[]{:S(2)}) collective-permute-start(f32[8,128]{1,0:T(8,128)S(1)} %broadcast_in_dim.5), channel_id=1, source_target_pairs={{0,16},{4,20},{8,24},{12,28},{16,0},{20,4},{24,8},{28,12},{32,48},... | collective-permute-start | bytes 12296 | tf_op jit(solution)/shard_map/ppermute | solution.py:130
  158.3 5.1 %collective-permute-start.11 = (f32[8,128]{1,0:T(8,128)S(1)}, f32[8,128]{1,0:T(8,128)S(1)}, u32[]{:S(2)}, u32[]{:S(2)}) collective-permute-start(f32[8,128]{1,0:T(8,128)S(1)} %broadcast_in_dim.5), channel_id=1, source_target_pairs={{0,8},{4,12},{8,16},{12,20},{16,24},{20,28},{24,0},{28,4},{32,40},... | collective-permute-start | bytes 12296 | tf_op jit(solution)/shard_map/ppermute | solution.py:130
  164.0 8.3 %collective-permute-start.16 = (f32[8,128]{1,0:T(8,128)S(1)}, f32[8,128]{1,0:T(8,128)S(1)}, u32[]{:S(2)}, u32[]{:S(2)}) collective-permute-start(f32[8,128]{1,0:T(8,128)S(1)} %maximum_maximum_fusion.1), channel_id=1, source_target_pairs={{0,96},{4,100},{8,104},{12,108},{16,112},{20,116},{24,120},{28,124... | collective-permute-start | bytes 12296 | tf_op jit(solution)/shard_map/ppermute | solution.py:130
  170.6 5.1 %collective-permute-start.15 = (f32[8,128]{1,0:T(8,128)S(1)}, f32[8,128]{1,0:T(8,128)S(1)}, u32[]{:S(2)}, u32[]{:S(2)}) collective-permute-start(f32[8,128]{1,0:T(8,128)S(1)} %maximum_maximum_fusion.1), channel_id=1, source_target_pairs={{0,64},{4,68},{8,72},{12,76},{16,80},{20,84},{24,88},{28,92},{32,9... | collective-permute-start | bytes 12296 | tf_op jit(solution)/shard_map/ppermute | solution.py:130
  171.3 4.8 %collective-permute-start.14 = (f32[8,128]{1,0:T(8,128)S(1)}, f32[8,128]{1,0:T(8,128)S(1)}, u32[]{:S(2)}, u32[]{:S(2)}) collective-permute-start(f32[8,128]{1,0:T(8,128)S(1)} %maximum_maximum_fusion.1), channel_id=1, source_target_pairs={{0,32},{4,36},{8,40},{12,44},{16,48},{20,52},{24,56},{28,60},{32,6... | collective-permute-start | bytes 12296 | tf_op jit(solution)/shard_map/ppermute | solution.py:130
  172.2 13.0 %collective-permute-start.10 = (f32[4,128,256]{2,1,0:T(8,128)S(1)}, f32[4,128,256]{2,1,0:T(8,128)S(1)}, u32[]{:S(2)}, u32[]{:S(2)}) collective-permute-start(f32[4,128,256]{2,1,0:T(8,128)S(1)} %get-tuple-element.31), channel_id=1, source_target_pairs={{0,1},{1,0},{2,3},{3,2},{4,5},{5,4},{6,7},{7,6},{8,9},{9,8},{10,11... | collective-permute-start | bytes 1572872 | tf_op jit(solution)/shard_map/ppermute | solution.py:144
  176.1 5.1 %collective-permute-start.17 = (f32[8,128]{1,0:T(8,128)S(1)}, f32[8,128]{1,0:T(8,128)S(1)}, u32[]{:S(2)}, u32[]{:S(2)}) collective-permute-start(f32[8,128]{1,0:T(8,128)S(1)} %maximum_maximum_fusion), channel_id=1, source_target_pairs={{0,4},{4,0},{8,12},{12,8},{16,20},{20,16},{24,28},{28,24},{32,36},... | collective-permute-start | bytes 12296 | tf_op jit(solution)/shard_map/ppermute | solution.py:130
  181.2 1.2 collective-permute-start.18
  181.3 5.2 %copy-start.21 = (f32[9,4,128,256]{3,2,1,0:T(8,128)}, f32[9,4,128,256]{3,2,1,0:T(8,128)S(1)}, u32[]{:S(2)}) copy-start(f32[9,4,128,256]{3,2,1,0:T(8,128)S(1)} %bitcast_dynamic-update-slice_fusion) | copy-start | bytes 14155780
